TPU v7x, 256 devices: a whole 4x4x8 slice. The times are simulated.
256 devices in a mesh: sub: 64 (over x, z, core), crs: 4 (over y).
Axes of the slice: x: 4, y: 4, z: 8, core: 2. Of those that a mesh axis runs over, the one named last changes fastest.
Arguments:
- residual: float32 [256, 6, 3072], P('sub', None, 'crs'), may hold values from -6 to 6
- stiffness: float32 [256, 6, 3072], P('sub', None, 'crs'), may hold values from 0.1 to 10
- solid: int32 [256, 6, 16], P('sub', None, 'crs'), may hold values 0 or 1
- inverses: bfloat16 [256, 6, 192, 3072], P('sub', None, None, 'crs')
- coarse_basis: bfloat16 [256, 24, 6, 3072], P('sub', None, None, 'crs'), may hold values from -0.29882812 to 0.29882812
- assign: int32 [256], replicated, may hold values from 0 to 255, as said below
- corners: int32 [256, 8], P('sub'), may hold values from 0 to 255, as said below
- coarse_inverse: float32 [768, 768], P('crs')
Outputs:
- preconditioned: float32 [256, 6, 3072], P('sub', None, 'crs')
- inner_value: float32 [1], replicated
Inputs may be any that keep to these rules, and one draw needn't show every extreme that they name: assign is a permutation of the 256 subdomain numbers, set at run time by the load balancer, so a subdomain's neighbours may be held on any devices. corners[t, c] is the number of corner c = 4 cx + 2 cy + cz of subdomain assign[t], the grid vertex at its place plus (cx, cy, cz) taken periodically, under one fixed permutation of the 256 vertices.
All inputs are finite; a program needn't handle non-finite values. No bound on the sum of `solid` on one device may be relied on, other than what follows from the above.
Results may differ from a plain program's by a relative error of at most 0.0028.
Values sent between devices are 32-bit elements; how exact they have to be, the bound alone decides.
No kernel may reach another device: no remote copies, remote signals or barrier semaphores. Data moves between devices by JAX's collectives and lax.ppermute only.
A program may use at most 128 MiB of HBM per device.

v0:
```python
import jax
import jax.numpy as jnp
from jax import lax
from jax.sharding import PartitionSpec as P


def partner_rows(assign, subs):
    depth = subs // 16
    slots = jnp.arange(subs, dtype=jnp.int32)
    inverse = jnp.sum(
        slots[:, None] * (assign[:, None] == slots[None, :]).astype(jnp.int32), axis=0
    )
    coord_a = assign // (4 * depth)
    coord_b = assign // depth % 4
    coord_c = assign % depth

    def number(first, second, third):
        return (first * 4 + second) * depth + third

    neighbours = jnp.stack(
        [
            number((coord_a + 1) % 4, coord_b, coord_c),
            number(coord_a, (coord_b + 1) % 4, coord_c),
            number(coord_a, coord_b, (coord_c + 1) % depth),
            number((coord_a + 3) % 4, coord_b, coord_c),
            number(coord_a, (coord_b + 3) % 4, coord_c),
            number(coord_a, coord_b, (coord_c + depth - 1) % depth),
        ],
        axis=1,
    )
    partner_slot = jnp.sum(
        inverse[None, None, :] * (neighbours[:, :, None] == slots[None, None, :]).astype(jnp.int32),
        axis=2,
    )
    partner_face = jnp.array([3, 4, 5, 0, 1, 2], dtype=jnp.int32)
    return (partner_slot * 6 + partner_face[None, :]).reshape(-1)


def body(residual, stiffness, solid, inverses, coarse_basis, assign, corners, coarse_inverse):
    slots_here, faces, width_here = residual.shape
    patches_here = solid.shape[2]
    entries = width_here // patches_here
    columns = lax.axis_size("crs")
    subs = assign.shape[0]
    face_rows = slots_here * faces
    rows = partner_rows(assign, subs)
    position = lax.axis_index("sub")
    own_rows = lax.dynamic_slice_in_dim(rows, position * face_rows, face_rows)
    flat_r = residual.reshape(face_rows, -1)
    flat_k = stiffness.reshape(face_rows, -1)
    solid_f = jnp.repeat(solid.astype(jnp.float32), entries, axis=2)
    all_r, all_k = (
        lax.all_gather(flat_r, "sub", axis=0, tiled=True),
        lax.all_gather(flat_k, "sub", axis=0, tiled=True),
    )
    partner_k = all_k[own_rows]
    weight = flat_k / (flat_k + partner_k)
    weight_partner = partner_k / (flat_k + partner_k)
    restricted_flat = weight * (flat_r + all_r[own_rows])
    restricted = (solid_f * restricted_flat.reshape(residual.shape)).astype(jnp.bfloat16)
    blocks = inverses.reshape(slots_here, faces, entries, patches_here, entries)
    vectors = restricted.reshape(slots_here, faces, patches_here, entries)
    local = jnp.einsum(
        "sfipj,sfpj->sfpi", blocks, vectors, preferred_element_type=jnp.float32
    ).reshape(residual.shape)
    coarse_part = jnp.einsum(
        "scfk,sfk->sc", coarse_basis, restricted, preferred_element_type=jnp.float32
    )
    total_coarse = 3 * subs
    index = (3 * corners[:, :, None] + jnp.arange(3, dtype=jnp.int32)[None, None, :]).reshape(
        slots_here, 24
    )
    onehot = (index[:, :, None] == jnp.arange(total_coarse, dtype=jnp.int32)[None, None, :]).astype(
        jnp.float32
    )
    coarse_local = jnp.einsum("sc,scn->n", coarse_part, onehot, precision=lax.Precision.HIGHEST)
    coarse_residual = lax.psum(coarse_local, ("sub", "crs"))
    block_width = total_coarse // columns
    start = lax.axis_index("crs") * block_width
    block_part = lax.dynamic_slice_in_dim(coarse_residual, start, block_width)
    terms = jnp.dot(block_part, coarse_inverse, precision=lax.Precision.HIGHEST)
    coarse_solution = lax.psum(terms, "crs")
    corner_values = jnp.einsum(
        "scn,n->sc", onehot, coarse_solution, precision=lax.Precision.HIGHEST
    ).astype(jnp.bfloat16)
    correction = jnp.einsum(
        "sc,scfk->sfk", corner_values, coarse_basis, preferred_element_type=jnp.float32
    )
    solution = solid_f * (local + correction)
    flat_u = solution.reshape(face_rows, -1)
    all_u = lax.all_gather(flat_u, "sub", axis=0, tiled=True)
    averaged = weight * flat_u + weight_partner * all_u[own_rows]
    preconditioned = averaged.reshape(residual.shape)
    inner_value = lax.psum(jnp.sum(residual * preconditioned), ("sub", "crs")).reshape(1)
    return (preconditioned, inner_value)


def solution(mesh):
    return jax.shard_map(
        body,
        mesh=mesh,
        in_specs=(
            P("sub", None, "crs"),
            P("sub", None, "crs"),
            P("sub", None, "crs"),
            P("sub", None, None, "crs"),
            P("sub", None, None, "crs"),
            P(),
            P("sub", None),
            P("crs", None),
        ),
        out_specs=(P("sub", None, "crs"), P()),
        check_vma=False,
    )
```

profile of v0, /device:TPU:1, one launch (start us, length us, event | category | flops | bytes accessed | tf_op | source)
XLA Modules:
  0.0 431.3 jit_solution(17880507166367437837)
XLA Ops:
  7.2 0.0 copy-start
  7.2 0.0 all-gather.4.cloned.1.call-start
  7.2 1.0 copy.44
  8.2 0.6 reshape.60
  8.8 0.0 all-gather.4.cloned.1.call-update
  8.9 0.0 all-gather.6.cloned.1.call-start
  8.9 0.9 copy.47
  9.8 0.6 reshape.62
  10.5 0.0 all-gather.6.cloned.1.call-update
  10.5 0.0 all-gather.8.cloned.1.call-start
  10.5 0.7 fusion.12
  11.3 0.8 select_reduce_fusion.1
  12.1 0.5 select_reduce_fusion
  12.6 0.7 multiply_add_fusion
  13.3 0.1 copy.42
  13.5 0.1 add.184
  13.6 0.7 convert_element_type.12
  14.3 0.1 copy.45
  14.4 0.1 broadcast_in_dim.5
  14.5 0.1 reshape.61
  14.7 11.4 %copy.63 = bf16[4,6,192,768]{2,3,1,0:T(8,128)(2,1)} copy(bf16[4,6,192,768]{3,2,1,0:T(8,128)(2,1)} %param.12) | data formatting | bytes 14155776 | tf_op jit(solution)/shard_map/reshape | solution.py:61
  26.1 0.1 add.189
  26.2 0.1 add.190
  26.3 0.1 add.192
  26.4 0.1 compare_select_fusion
  26.4 68.0 %all-gather.4.cloned.1.call-done = f32[1536,768]{1,0:T(8,128)} async-done(((f32[24,768]{1,0:T(8,128)}), f32[1536,768]{1,0:T(8,128)}) %all-gather.4.cloned.1.call-update) | async-done | bytes 4718608 | tf_op jit(solution)/shard_map/all_gather | solution.py:54
  94.5 3.0 gather_fusion
  97.5 77.1 %all-gather.6.cloned.1.call-done = f32[1536,768]{1,0:T(8,128)} async-done(((f32[24,768]{1,0:T(8,128)}), f32[1536,768]{1,0:T(8,128)}) %all-gather.6.cloned.1.call-update) | async-done | bytes 4718608 | tf_op jit(solution)/shard_map/all_gather | solution.py:53
  174.5 3.0 gather_fusion.1
  177.5 0.1 fusion.3
  177.6 0.1 reshape.108
  177.7 5.1 %fusion.25 = f32[4,6,4,1,192]{4,3,2,1,0:T(1,128)S(1)} fusion(bf16[4,6,4,192,1]{3,4,2,1,0:T(2,128)(2,1)S(1)} %reshape.108, bf16[4,6,192,4,192]{2,4,3,1,0:T(8,128)(2,1)} %bitcast.41), kind=kOutput, calls=%fused_computation.85 | convolution fusion | flops 7077888 | bytes 7188480 | tf_op jit(solution)/shard_map/sfipj,sfpj->sfpi/dot_general | solution.py:63
  182.9 0.1 reshape.65
  183.0 0.4 convolution_bitcast_fusion
  183.4 0.3 convolution_reduce_fusion.1
  183.7 75.2 %psum.21 = f32[768]{0:T(1024)S(1)} all-reduce(f32[768]{0:T(1024)S(1)} %convolution_reduce_fusion.1), channel_id=1, replica_groups=mesh['sub'=64,'crs'=4] {'sub','crs'}, use_global_device_ids=true, to_apply=%region_2.3 | all-reduce | flops 768 | bytes 6144 | tf_op jit(solution)/shard_map/psum | solution.py:77
  258.9 0.1 dynamic_slice.7
  259.0 0.4 convolution_reduce_fusion
  259.4 7.2 %psum.22 = f32[768]{0:T(1024)S(1)} all-reduce(f32[768]{0:T(1024)S(1)} %convolution_reduce_fusion), channel_id=1, replica_groups=mesh['sub'=64,'crs'=4] {'crs'}, use_global_device_ids=true, to_apply=%region_3.4 | all-reduce | flops 768 | bytes 6144 | tf_op jit(solution)/shard_map/psum | solution.py:82
  266.6 0.5 fusion
  267.2 0.3 fusion.7
  267.5 0.6 reshape.66
  268.1 0.0 all-gather.8.cloned.1.call-update
  268.2 77.2 %all-gather.8.cloned.1.call-done = f32[1536,768]{1,0:T(8,128)} async-done(((f32[24,768]{1,0:T(8,128)}), f32[1536,768]{1,0:T(8,128)}) %all-gather.8.cloned.1.call-update) | async-done | bytes 4718608 | tf_op jit(solution)/shard_map/all_gather | solution.py:91
  345.4 3.0 gather_fusion.2
  348.3 0.7 multiply_reduce_fusion
  349.0 0.7 copy.53
  349.7 75.1 %psum.23 = f32[1]{0:T(128)} all-reduce(f32[1]{0:T(128)} %bitcast.18), channel_id=1, replica_groups=mesh['sub'=64,'crs'=4] {'sub','crs'}, use_global_device_ids=true, to_apply=%region_5.6 | all-reduce | flops 1 | bytes 8 | tf_op jit(solution)/shard_map/psum | solution.py:94
  (22 shorter events, 0.2 us)
Async XLA Ops:
  7.2 175.8 %copy-start = (bf16[4,24,6,768]{3,1,2,0:T(8,128)(2,1)S(1)}, bf16[4,24,6,768]{3,1,2,0:T(8,128)(2,1)}, u32[]{:S(2)}) copy-start(bf16[4,24,6,768]{3,1,2,0:T(8,128)(2,1)} %param.13) | copy-start | bytes 2654212
  7.2 87.3 %all-gather.4.cloned.1.call-start = ((), (), s32[]{:S(2)}) async-start(), calls=%async_computation | async-start | bytes 4792320 | tf_op jit(solution)/shard_map/all_gather | solution.py:54
  8.9 165.7 %all-gather.6.cloned.1.call-start = ((), (), s32[]{:S(2)}) async-start(), calls=%async_computation.1 | async-start | bytes 4792320 | tf_op jit(solution)/shard_map/all_gather | solution.py:53
  10.5 334.9 %all-gather.8.cloned.1.call-start = ((), (), s32[]{:S(2)}) async-start(), calls=%async_computation.2 | async-start | bytes 4792320 | tf_op jit(solution)/shard_map/all_gather | solution.py:91
  14.7 11.4 %copy-start.4 = (s32[4,8]{1,0:T(4,128)S(1)}, s32[4,8]{1,0:T(4,128)}, u32[]{:S(2)}) copy-start(s32[4,8]{1,0:T(4,128)} %param.15) | copy-start | bytes 388
  14.7 162.9 %copy-start.1 = (f32[4,6,768]{2,0,1:T(4,128)S(1)}, f32[4,6,768]{2,0,1:T(4,128)}, u32[]{:S(2)}) copy-start(f32[4,6,768]{2,0,1:T(4,128)} %param.9) | copy-start | bytes 221188
  14.7 162.9 %copy-start.2 = (f32[4,6,768]{2,0,1:T(4,128)S(1)}, f32[4,6,768]{2,0,1:T(4,128)}, u32[]{:S(2)}) copy-start(f32[4,6,768]{2,0,1:T(4,128)} %param.10) | copy-start | bytes 221188
  177.7 81.3 %copy-start.3 = (f32[192,768]{1,0:T(8,128)S(1)}, f32[192,768]{1,0:T(8,128)}, u32[]{:S(2)}) copy-start(f32[192,768]{1,0:T(8,128)} %param.16) | copy-start | bytes 1769476
Sparse Core Ops, SparseCore 0:
  10.8 83.6 all-gather.3
  97.8 76.6 all-gather.5
  268.3 77.0 all-gather.7
where the time goes:
time: 432 us; the launch traced here: 431 us
  waiting for transfers between devices  222 us (51%)
  blocking collectives  158 us (37%)
  local copies, waits for them, and re-layouts  26 us (6%)
  between operations  14 us (3%)
  matrix products  7.02 us (2%)
    all_gather x1, waiting for transfers between devices, body(): all_u = lax.all_gather(flat_u, 'sub', axis=0, tiled=True)  77.2 us
    all_gather x1, waiting for transfers between devices, body(): lax.all_gather(flat_r, 'sub', axis=0, tiled=True)  77.1 us
    psum x1, blocking collectives, body(): coarse_residual = lax.psum(coarse_local, ('sub', 'crs'))  75.2 us
    psum x1, blocking collectives, body(): lax.psum(jnp.sum(residual * preconditioned), ('sub', 'crs')).reshape(1)  75.1 us
    all_gather x1, waiting for transfers between devices, body(): lax.all_gather(flat_k, 'sub', axis=0, tiled=True)  68 us
    reshape x1, local copies, waits for them, and re-layouts, body(): blocks = inverses.reshape(slots_here, faces, entries, patches_here, entries)  11.4 us
  transfers between devices with their start and end apart: 3, of which 3 were waited for; matrix products, arithmetic and copies ran while one was open for 5% of the time, Pallas kernels for 0%

commit v1 on v0

v1 whole, which is shorter than its diff:
```python
import jax
import jax.numpy as jnp
from jax import lax
from jax.experimental import pallas as pl
from jax.experimental.pallas import tpu as pltpu
from jax.sharding import PartitionSpec as P


F32 = jnp.float32
BF16 = jnp.bfloat16
VMEM = pltpu.VMEM
SMEM = pltpu.SMEM


def iota(shape, axis):
    return lax.broadcasted_iota(jnp.int32, shape, axis)


def pair_transpose(first, second):
    both = jnp.concatenate([first, second], axis=1)
    turned = both.T
    return turned[:64], turned[64:]


def stack_rows(faces, k):
    return jnp.concatenate(
        [
            faces[s][:, p * 192 + k * 64 : p * 192 + k * 64 + 64]
            for s in range(4)
            for p in range(4)
        ],
        axis=0,
    )


def slot_faces(ref, s, pads):
    return jnp.concatenate([ref[f, s : s + 1, :] for f in range(6)] + pads, axis=0)


def unpack_faces(tiles):
    first = jnp.concatenate([tiles[0], tiles[1]], axis=0).T
    second = jnp.concatenate([tiles[2], jnp.zeros_like(tiles[2])], axis=0).T
    faces = []
    for s in range(4):
        pieces = []
        for p in range(4):
            row = s * 32 + p * 8
            pieces += [first[row : row + 8], second[row : row + 8, :64]]
        faces.append(jnp.concatenate(pieces, axis=1))
    return faces


def to_slots(tiles):
    pad = jnp.zeros((64, 32), F32)
    return jnp.concatenate(
        [
            jnp.concatenate([tile[:, s * 32 : s * 32 + 32] for tile in tiles] + [pad], axis=1)
            for s in range(4)
        ],
        axis=0,
    )


def from_slots(rows, k):
    return jnp.concatenate(
        [rows[s * 64 : s * 64 + 64, k * 32 : k * 32 + 32] for s in range(4)], axis=1
    )


def select_rows(onehot, values):
    high = values.astype(BF16)
    rest = values - high.astype(F32)
    middle = rest.astype(BF16)
    low = (rest - middle.astype(F32)).astype(BF16)
    width = values.shape[1]
    parts = jnp.concatenate([high, middle, low], axis=1)
    out = jnp.dot(onehot, parts, preferred_element_type=F32)
    return (out[:, :width] + out[:, width : 2 * width]) + out[:, 2 * width :]


def rows_ahead(values, count):
    return pltpu.roll(values, (-count) % 256, 0)


def lanes_ahead(values, count):
    return pltpu.roll(values, (-count) % values.shape[1], 1)


def step_forward(values, direction):
    row = iota(values.shape, 0)
    if direction == 0:
        return rows_ahead(values, 64)
    if direction == 1:
        return jnp.where(row // 16 % 4 == 3, rows_ahead(values, -48), rows_ahead(values, 16))
    return jnp.where(row % 16 == 15, rows_ahead(values, -15), rows_ahead(values, 1))


def step_back(values, direction):
    row = iota(values.shape, 0)
    if direction == 0:
        return rows_ahead(values, -64)
    if direction == 1:
        return jnp.where(row // 16 % 4 == 0, rows_ahead(values, 48), rows_ahead(values, -16))
    return jnp.where(row % 16 == 0, rows_ahead(values, 15), rows_ahead(values, -1))


def partner(values):
    face = iota(values.shape, 1) % 8
    minus = lanes_ahead(values, 3)
    plus = lanes_ahead(values, -3)
    out = step_forward(minus, 0)
    out = jnp.where(face == 1, step_forward(minus, 1), out)
    out = jnp.where(face == 2, step_forward(minus, 2), out)
    out = jnp.where(face == 3, step_back(plus, 0), out)
    out = jnp.where(face == 4, step_back(plus, 1), out)
    return jnp.where(face == 5, step_back(plus, 2), out)


def pack_kernel(assign_ref, corners_ref, residual_ref, stiffness_ref, out_ref):
    res = []
    stiff = []
    ones = jnp.ones((1, 768), F32)
    for s in range(4):
        vertex = jnp.full((1, 768), corners_ref[s, 0].astype(F32), F32)
        place = jnp.full((1, 768), assign_ref[s].astype(F32), F32)
        res.append(slot_faces(residual_ref, s, [vertex, place]))
        stiff.append(slot_faces(stiffness_ref, s, [ones, ones]))
    pairs = [((res, 0), (res, 1)), ((res, 2), (stiff, 0)), ((stiff, 1), (stiff, 2))]
    for at, (one, two) in enumerate(pairs):
        a, b = pair_transpose(stack_rows(*one), stack_rows(*two))
        out_ref[:, 0, at * 256 : at * 256 + 128] = a
        out_ref[:, 0, at * 256 + 128 : at * 256 + 256] = b


def weigh_kernel(in_ref, out_ref, weight_ref, weight_partner_ref, place_ref, slot_ref, vertex_ref):
    tiles = [in_ref[:, 0, at * 128 : at * 128 + 128] for at in range(6)]
    res = to_slots(tiles[:3])
    stiff = to_slots(tiles[3:])
    lane = iota((256, 256), 1).astype(F32)
    to_place = jnp.where(res[:, 7:8] == lane, 1.0, 0.0).astype(F32)
    from_place = to_place.astype(BF16)
    to_place = to_place.T.astype(BF16)
    both = select_rows(to_place, jnp.concatenate([res, stiff], axis=1))
    res = both[:, :128]
    stiff = both[:, 128:]
    vertex = jnp.broadcast_to(res[:, 6:7], (256, 128)).T[0:1, :]
    entry_vertex = (iota((768, 1), 0) // 3).astype(F32)
    stiff_partner = partner(stiff)
    total = stiff + stiff_partner
    weight = stiff / total
    back = select_rows(from_place, weight * (res + partner(res)))
    for k in range(3):
        out_ref[:, 0, k * 128 : k * 128 + 128] = from_slots(back, k)
    weight_ref[...] = weight
    weight_partner_ref[...] = stiff_partner / total
    place_ref[...] = to_place
    slot_ref[...] = from_place
    vertex_ref[...] = jnp.where(entry_vertex == vertex, 1.0, 0.0).astype(BF16)


def face_mask(shape, index):
    lane = iota(shape, 1)
    return (lane // 32 == index // 6) & (lane % 8 == index % 6)


def solve_kernel(group, in_ref, solid_ref, inverses_ref, basis_ref, local_ref, message_ref, rhs, total):
    step = pl.program_id(0)
    tiles = [in_ref[:, 0, k * 128 : k * 128 + 128] for k in range(3)]

    @pl.when(step == 0)
    def _():
        patch = iota((64, 128), 1) // 8 % 4
        for k in range(3):
            value = tiles[k] * solid_ref[...]
            for p in range(4):
                row = p * 192 + k * 64
                rhs[row : row + 64, :] = jnp.where(patch == p, value, 0.0).astype(BF16)
        total[...] = jnp.zeros_like(total)

    product = jnp.dot(inverses_ref[...], rhs[...], preferred_element_type=F32)
    held = total[...]
    for at in range(group):
        mask = face_mask((192, 128), step * group + at)
        held = jnp.where(mask, product[at * 192 : at * 192 + 192], held)
    total[...] = held

    @pl.when(step == pl.num_programs(0) - 1)
    def _():
        coarse = jnp.dot(basis_ref[...], rhs[...], preferred_element_type=F32)
        parts = []
        for s in range(4):
            part = jnp.zeros((24, 128), F32)
            for f in range(6):
                at = s * 6 + f
                part = part + jnp.where(
                    face_mask((24, 128), at), coarse[at * 24 : at * 24 + 24], 0.0
                )
            parts += [part, jnp.zeros((8, 128), F32)]
        row = jnp.sum(jnp.concatenate(parts, axis=0).T, axis=0, keepdims=True)
        product_sum = jnp.zeros((64, 128), F32)
        for k in range(3):
            product_sum = product_sum + tiles[k] * held[k * 64 : k * 64 + 64]
        inner = jnp.sum(
            jnp.sum(product_sum, axis=0, keepdims=True) * solid_ref[...], axis=1, keepdims=True
        )
        row = jnp.where(iota((1, 128), 1) == 24, inner, row)
        message_ref[...] = jnp.broadcast_to(row.reshape(1, 1, 128), message_ref.shape)
        local_ref[...] = held


def coarse_kernel(
    corners_ref, in_ref, place_ref, vertex_ref, inverse_ref, basis_ref, local_ref, solid_ref,
    out_ref, inner_ref,
):
    summed = in_ref[0:64, 0, :]
    for y in range(1, 4):
        summed = summed + in_ref[y * 64 : y * 64 + 64, 0, :]
    inner = jnp.sum(jnp.sum(summed, axis=0, keepdims=True)[:, 24:25], axis=1, keepdims=True)
    pad = jnp.zeros((64, 96), F32)
    parts = jnp.concatenate(
        [jnp.concatenate([summed[:, s * 32 : s * 32 + 32], pad], axis=1) for s in range(4)], axis=0
    )
    parts = select_rows(place_ref[...], parts)
    for direction, count in ((2, 3), (1, 6), (0, 12)):
        parts = parts + step_back(lanes_ahead(parts, count), direction)
    by_entry = select_rows(vertex_ref[...], parts)
    own = iota((768, 128), 0) % 3 == iota((768, 128), 1)
    column = jnp.sum(jnp.where(own, by_entry, 0.0), axis=1, keepdims=True)
    solution = jnp.sum(inverse_ref[...] * column, axis=0, keepdims=True)
    diagonal = iota((768, 768), 0) == iota((768, 768), 1)
    residual = jnp.sum(jnp.where(diagonal, column, 0.0), axis=0, keepdims=True)
    rounded = solution.astype(BF16).astype(F32)
    inner_ref[...] = inner + jnp.sum(rounded * residual, axis=1, keepdims=True)
    entry = iota((24, 768), 0)
    lane = iota((24, 768), 1)
    faces = []
    for s in range(4):
        index = entry % 3
        for c in range(8):
            index = jnp.where(entry // 3 == c, entry % 3 + 3 * corners_ref[s, c], index)
        values = jnp.sum(jnp.where(lane == index, rounded, 0.0), axis=1, keepdims=True)
        rows = []
        for f in range(6):
            block = basis_ref[(s * 6 + f) * 24 : (s * 6 + f) * 24 + 24, :].astype(F32)
            rows.append(jnp.sum(block * values, axis=0, keepdims=True))
        faces.append(jnp.concatenate(rows + [jnp.zeros((2, 768), F32)], axis=0))
    a, b = pair_transpose(stack_rows(faces, 0), stack_rows(faces, 1))
    c, _ = pair_transpose(stack_rows(faces, 2), jnp.zeros((128, 64), F32))
    for k, tile in enumerate((a, b, c)):
        out_ref[:, 0, k * 128 : k * 128 + 128] = solid_ref[...] * (
            local_ref[k * 64 : k * 64 + 64] + tile
        )


def average_kernel(in_ref, place_ref, slot_ref, weight_ref, weight_partner_ref, out_ref):
    tiles = [in_ref[:, 0, k * 128 : k * 128 + 128] for k in range(3)]
    values = select_rows(place_ref[...], to_slots(tiles))
    values = weight_ref[...] * values + weight_partner_ref[...] * partner(values)
    back = select_rows(slot_ref[...], values)
    for k in range(3):
        out_ref[:, 0, k * 128 : k * 128 + 128] = from_slots(back, k)


def unpack_kernel(in_ref, out_ref):
    faces = unpack_faces([in_ref[:, 0, k * 128 : k * 128 + 128] for k in range(3)])
    for f in range(6):
        out_ref[f] = jnp.concatenate([faces[s][f : f + 1, :] for s in range(4)], axis=0)


def spec(space=VMEM):
    return pl.BlockSpec(memory_space=space)


def shaped(*shape, dtype=F32):
    return jax.ShapeDtypeStruct(shape, dtype)


def call(kernel, inputs, outputs, name):
    return pl.pallas_call(
        kernel,
        in_specs=[spec(space) for space in inputs],
        out_specs=tuple(spec() for _ in outputs),
        out_shape=tuple(outputs),
        name=name,
        compiler_params=pltpu.CompilerParams(vmem_limit_bytes=24 * 2**20),
    )


def exchange(values, axes):
    return lax.all_to_all(values, axes, 0, 0)


def body(residual, stiffness, solid, inverses, coarse_basis, assign, corners, coarse_inverse):
    full_inverse = lax.all_gather(coarse_inverse, "crs", axis=0, tiled=True)
    mine = lax.dynamic_slice_in_dim(assign, 4 * lax.axis_index("sub"), 4)
    solid_row = jnp.pad(
        solid.transpose(0, 2, 1).astype(F32), ((0, 0), (0, 0), (0, 2))
    ).reshape(1, 128)
    basis_rows = coarse_basis.transpose(0, 2, 1, 3).reshape(576, 768)

    (packed,) = call(pack_kernel, [SMEM, SMEM, VMEM, VMEM], [shaped(64, 1, 768)], "pack")(
        mine, corners, residual.transpose(1, 0, 2), stiffness.transpose(1, 0, 2)
    )
    weighed, weight, weight_partner, to_place, from_place, to_vertex = call(
        weigh_kernel,
        [VMEM],
        [shaped(64, 1, 384), shaped(256, 128), shaped(256, 128)]
        + [shaped(n, 256, dtype=BF16) for n in (256, 256, 768)],
        "weigh",
    )(exchange(packed, "sub"))

    group = 4
    local, message = pl.pallas_call(
        lambda *refs: solve_kernel(group, *refs),
        grid=(24 // group,),
        in_specs=[
            pl.BlockSpec((64, 1, 384), lambda i: (0, 0, 0)),
            pl.BlockSpec((1, 128), lambda i: (0, 0)),
            pl.BlockSpec((group * 192, 768), lambda i: (i, 0)),
            pl.BlockSpec((576, 768), lambda i: (0, 0)),
        ],
        out_specs=(
            pl.BlockSpec((192, 128), lambda i: (0, 0)),
            pl.BlockSpec((256, 1, 128), lambda i: (0, 0, 0)),
        ),
        out_shape=(shaped(192, 128), shaped(256, 1, 128)),
        scratch_shapes=[pltpu.VMEM((768, 128), BF16), pltpu.VMEM((192, 128), F32)],
        name="solve",
        compiler_params=pltpu.CompilerParams(vmem_limit_bytes=24 * 2**20),
    )(exchange(weighed, "sub"), solid_row, inverses.reshape(4608, 768), basis_rows)

    solved, inner = call(
        coarse_kernel,
        [SMEM] + [VMEM] * 7,
        [shaped(64, 1, 384), shaped(1, 1)],
        "coarse",
    )(
        corners,
        exchange(message, ("crs", "sub")),
        to_place,
        to_vertex,
        full_inverse,
        basis_rows,
        local,
        solid_row,
    )
    (averaged,) = call(average_kernel, [VMEM] * 5, [shaped(64, 1, 384)], "average")(
        exchange(solved, "sub"), to_place, from_place, weight, weight_partner
    )
    (out,) = call(unpack_kernel, [VMEM], [shaped(6, 4, 768)], "unpack")(exchange(averaged, "sub"))
    return out.transpose(1, 0, 2), inner.reshape(1)


def solution(mesh):
    return jax.shard_map(
        body,
        mesh=mesh,
        in_specs=(
            P("sub", None, "crs"),
            P("sub", None, "crs"),
            P("sub", None, "crs"),
            P("sub", None, None, "crs"),
            P("sub", None, None, "crs"),
            P(),
            P("sub", None),
            P("crs", None),
        ),
        out_specs=(P("sub", None, "crs"), P()),
        check_vma=False,
    )
```

time: 432 us -> 123 us (0.28)
  waiting for transfers between devices: 222 us -> 10 us
  blocking collectives: 158 us -> 72.2 us
  local copies, waits for them, and re-layouts: 26 us -> 9.15 us
  Pallas kernels: 0 us -> 10.8 us
  matrix products: 7.02 us -> 0 us
  starting transfers between devices: 0.12 us -> 5.73 us
    all_gather x3 -> x1, waiting for transfers between devices: 222 us -> 0.01 us  [body(): full_inverse = lax.all_gather(coarse_inverse, 'crs', axis=0, tiled=True)]
    psum x3 -> x0, blocking collectives: 158 us -> none  [the longest x1 75.2 us: body(): coarse_residual = lax.psum(coarse_local, ('sub', 'crs'))]
    all_to_all x0 -> x4, blocking collectives: none -> 72.2 us  [exchange(): return lax.all_to_all(values, axes, 0, 0)]
    reshape x7 -> x1, local copies, waits for them, and re-layouts: 13.7 us -> 0.09 us  [body(): solid_row = jnp.pad(solid.transpose(0, 2, 1).astype(F32), ((0, 0), (0, 0)...]
    pallas_call x0 -> x6, Pallas kernels: none -> 10.8 us  [the longest x1 3.83 us: body(): pl.pallas_call(lambda *refs: solve_kernel(group, *refs), grid=(24 // grou...]
    all_to_all x0 -> x1, waiting for transfers between devices: none -> 9.36 us  [exchange(): return lax.all_to_all(values, axes, 0, 0)]
    gather x6 -> x0, local copies, waits for them, and re-layouts: 8.92 us -> none  [the longest x2 2.97 us: body(): averaged = weight * flat_u + weight_partner * all_u[own_rows]]
    dot_general x6 -> x0, matrix products: 7.02 us -> none  [the longest x1 5.08 us: body(): jnp.einsum('sfipj,sfpj->sfpi', blocks, vectors, preferred_element_type=jn...]
  transfers between devices with their start and end apart: 3 -> 2, of which waited for: 3 -> 1; matrix products, arithmetic and copies ran while one was open for 5% -> 1% of each run, Pallas kernels for 0% -> 5%
where the time goes in v1:
time: 123 us
  blocking collectives  72.2 us (59%)
  between operations  14.1 us (11%)
  Pallas kernels  10.8 us (9%)
  waiting for transfers between devices  10 us (8%)
  local copies, waits for them, and re-layouts  9.15 us (7%)
  starting transfers between devices  5.73 us (5%)
    all_to_all x4, blocking collectives, exchange(): return lax.all_to_all(values, axes, 0, 0)  72.2 us
    all_to_all x1, waiting for transfers between devices, exchange(): return lax.all_to_all(values, axes, 0, 0)  9.36 us
    unnamed x16, local copies, waits for them, and re-layouts  8.3 us
    all_to_all x1, starting transfers between devices, exchange(): return lax.all_to_all(values, axes, 0, 0)  5.7 us
    pallas_call x1, Pallas kernels, body(): pl.pallas_call(lambda *refs: solve_kernel(group, *refs), grid=(24 // grou...  3.83 us
    pallas_call x1, Pallas kernels, body(): call(coarse_kernel, [SMEM] + [VMEM] * 7, [shaped(64, 1, 384), shaped(1, 1...  2.57 us
  transfers between devices with their start and end apart: 2, of which 1 were waited for; matrix products, arithmetic and copies ran while one was open for 1% of the time, Pallas kernels for 5%

profile of v1, /device:TPU:1, one launch (start us, length us, event | category | flops | bytes accessed | tf_op | source)
XLA Modules:
  0.0 122.7 jit_solution(3287706690111134446)
XLA Ops:
  7.2 0.0 copy-start.2
  7.2 0.0 all-gather.2.cloned.1.call-start
  7.2 0.7 all-gather.2.cloned.1.call-update
  7.9 0.8 dynamic_slice.3.assign_ref
  8.7 0.0 copy-start.4
  8.7 0.9 copy-done.4
  9.6 0.0 copy-start.5
  9.6 0.9 copy-done.5
  10.4 0.0 copy-start.6
  10.4 0.7 copy-done.6
  11.1 0.0 copy-start.7
  11.1 0.9 pack.1
  12.0 23.7 %all_to_all.25.in_ref = f32[64,1,768]{2,1,0:T(1,128)S(1)} all-to-all(f32[64,1,768]{2,1,0:T(1,128)S(1)} %pack.1), channel_id=1, replica_groups=mesh['sub'=64,'crs'=4] {'sub'}, dimensions={0} | all-to-all | bytes 393216 | tf_op jit(solution)/shard_map/all_to_all | solution.py:290
  35.7 1.9 %weigh.1 = (f32[64,1,384]{2,1,0:T(1,128)}, f32[256,128]{1,0:T(8,128)S(1)}, f32[256,128]{1,0:T(8,128)S(1)}, bf16[256,256]{1,0:T(8,128)(2,1)S(1)}, bf16[256,256]{1...) custom-call(f32[64,1,768]{2,1,0:T(1,128)S(1)} %all_to_all.25.in_ref), custom_call_target="tpu_custom_call" | custom-call | tf_op jit(solution)/shard_map/weigh/pallas_call | solution.py:304
  37.6 5.7 %all-to-all-start.1 = ((f32[64,1,384]{2,1,0:T(1,128)}), f32[64,1,384]{2,1,0:T(1,128)S(1)}, u32[]{:S(2)}, u32[]{:S(2)}) async-start(f32[64,1,384]{2,1,0:T(1,128)} %get-tuple-element.12), calls=%async_computation.1 | async-start | bytes 196608 | tf_op jit(solution)/shard_map/all_to_all | solution.py:290
  43.3 0.7 convert_bitcast_fusion
  44.0 0.1 reshape.16.refs_1_.solid_ref
  44.1 9.4 %all-to-all-done.1.refs_0_ = f32[64,1,384]{2,1,0:T(1,128)S(1)} async-done(((f32[64,1,384]{2,1,0:T(1,128)}), f32[64,1,384]{2,1,0:T(1,128)S(1)}, u32[]{:S(2)}, u32[]{:S(2)}) %all-to-all-start.1) | async-done | bytes 98336 | tf_op jit(solution)/shard_map/all_to_all | solution.py:290
  53.5 0.0 copy-start
  53.5 3.0 %copy-done = bf16[4,6,192,768]{3,2,1,0:T(8,128)(2,1)S(1)} copy-done((bf16[4,6,192,768]{3,2,1,0:T(8,128)(2,1)S(1)}, bf16[4,6,192,768]{3,2,1,0:T(8,128)(2,1)}, u32[]{:S(2)}) %copy-start) | copy-done | bytes 7077912
  56.5 0.0 copy-start.1
  56.5 1.2 copy-done.1
  57.7 3.8 %solve.1 = (f32[192,128]{1,0:T(8,128)S(1)}, f32[256,1,128]{2,1,0:T(1,128)S(1)}) custom-call(f32[64,1,384]{2,1,0:T(1,128)S(1)} %all-to-all-done.1.refs_0_, f32[1,128]{1,0:T(1,128)S(1)} %reshape.16.refs_1_.solid_ref, bf16[4608,768]{1,0:T(8,128)(2,1)S(1)} %bitcast.10, bf16[576,768]{1,0:T(8,128)(2,1)S(1)} %bitcast.11), custom_call_target="tpu_custom_call" | custom-call | tf_op jit(solution)/shard_map/solve/pallas_call | solution.py:313
  61.5 19.7 %all_to_all.26.in_ref = f32[256,1,128]{2,1,0:T(1,128)S(1)} all-to-all(f32[256,1,128]{2,1,0:T(1,128)S(1)} %get-tuple-element.13), channel_id=1, replica_groups=mesh['sub'=64,'crs'=4] {'crs','sub'}, dimensions={0} | all-to-all | bytes 262144 | tf_op jit(solution)/shard_map/all_to_all | solution.py:290
  81.2 0.0 all-gather.2.cloned.1.call-done.inverse_ref
  81.2 0.0 copy-done.2
  81.3 0.0 copy-done.7
  81.3 0.0 copy-start.3
  81.3 1.7 %copy-done.3 = f32[768,768]{1,0:T(8,128)S(1)} copy-done((f32[768,768]{1,0:T(8,128)S(1)}, f32[768,768]{1,0:T(8,128)}, u32[]{:S(2)}) %copy-start.3) | copy-done | bytes 2359320
  82.9 2.6 %coarse.1 = (f32[64,1,384]{2,1,0:T(1,128)S(1)}, f32[1,1]{1,0:T(1,128)}) custom-call(s32[4,8]{1,0:T(4,128)S(1)} %copy-done.7, f32[256,1,128]{2,1,0:T(1,128)S(1)} %all_to_all.26.in_ref, bf16[256,256]{1,0:T(8,128)(2,1)S(1)} %get-tuple-element.14.place_ref, bf16[768,256]{1,0:T(8,128)(2,1)S(1)} %get-tuple-element.15.vertex_ref, f32[768,768]{1,0:T(8,128)S(1)} %copy-done.3, ...), custom_call_target="tpu_custom_call" | custom-call | tf_op jit(solution)/shard_map/coarse/pallas_call | solution.py:332
  85.5 14.4 %all_to_all.27.in_ref = f32[64,1,384]{2,1,0:T(1,128)S(1)} all-to-all(f32[64,1,384]{2,1,0:T(1,128)S(1)} %get-tuple-element.17), channel_id=1, replica_groups=mesh['sub'=64,'crs'=4] {'sub'}, dimensions={0} | all-to-all | bytes 196608 | tf_op jit(solution)/shard_map/all_to_all | solution.py:290
  99.9 0.8 average.1
  100.7 14.3 %all_to_all.28.in_ref = f32[64,1,384]{2,1,0:T(1,128)S(1)} all-to-all(f32[64,1,384]{2,1,0:T(1,128)S(1)} %average.1), channel_id=1, replica_groups=mesh['sub'=64,'crs'=4] {'sub'}, dimensions={0} | all-to-all | bytes 196608 | tf_op jit(solution)/shard_map/all_to_all | solution.py:290
  115.0 0.8 unpack.1
  (1 shorter events, 0.0 us)
Async XLA Ops:
  7.2 74.1 %copy-start.2 = (bf16[4,24,6,768]{3,1,2,0:T(8,128)(2,1)S(1)}, bf16[4,24,6,768]{3,1,2,0:T(8,128)(2,1)}, u32[]{:S(2)}) copy-start(bf16[4,24,6,768]{3,1,2,0:T(8,128)(2,1)} %param.12) | copy-start | bytes 2654212
  7.2 74.1 %all-gather.2.cloned.1.call-start = ((), (), s32[]{:S(2)}) async-start(), calls=%async_computation.5 | async-start | bytes 2949120 | tf_op jit(solution)/shard_map/all_gather | solution.py:294
  8.7 0.9 copy-start.4
  9.6 0.9 copy-start.5
  10.4 0.7 copy-start.6
  11.1 70.1 %copy-start.7 = (s32[4,8]{1,0:T(4,128)S(1)}, s32[4,8]{1,0:T(4,128)}, u32[]{:S(2)}) copy-start(s32[4,8]{1,0:T(4,128)} %corners_ref.3) | copy-start | bytes 388
  37.6 15.9 %all-to-all-start.1 = ((f32[64,1,384]{2,1,0:T(1,128)}), f32[64,1,384]{2,1,0:T(1,128)S(1)}, u32[]{:S(2)}, u32[]{:S(2)}) async-start(f32[64,1,384]{2,1,0:T(1,128)} %get-tuple-element.12), calls=%async_computation.1 | async-start | bytes 196608 | tf_op jit(solution)/shard_map/all_to_all | solution.py:290
  53.5 3.0 %copy-start = (bf16[4,6,192,768]{3,2,1,0:T(8,128)(2,1)S(1)}, bf16[4,6,192,768]{3,2,1,0:T(8,128)(2,1)}, u32[]{:S(2)}) copy-start(bf16[4,6,192,768]{3,2,1,0:T(8,128)(2,1)} %param.11) | copy-start | bytes 21233668
  56.5 1.2 copy-start.1
  81.3 1.7 %copy-start.3 = (f32[768,768]{1,0:T(8,128)S(1)}, f32[768,768]{1,0:T(8,128)}, u32[]{:S(2)}) copy-start(f32[768,768]{1,0:T(8,128)} %all-gather.2.cloned.1.call-done.inverse_ref) | copy-start | bytes 7077892
Sparse Core Ops, SparseCore 0:
  9.8 39.3 all-gather.1

commit v2 on v1

--- a/solution.py
+++ b/solution.py
@@ -10,6 +10,7 @@
 BF16 = jnp.bfloat16
 VMEM = pltpu.VMEM
 SMEM = pltpu.SMEM
+HBM = pltpu.HBM
 
 
 def iota(shape, axis):
@@ -116,20 +117,46 @@
     return jnp.where(face == 5, step_back(plus, 2), out)
 
 
-def pack_kernel(assign_ref, corners_ref, residual_ref, stiffness_ref, out_ref):
+def fetch(sources, targets, sems):
+    copies = [
+        pltpu.make_async_copy(source, target, sems.at[at])
+        for at, (source, target) in enumerate(zip(sources, targets))
+    ]
+    for copy in copies:
+        copy.start()
+    return copies
+
+
+def pack_kernel(
+    assign_hbm, corners_hbm, solid_hbm, residual_hbm, stiffness_hbm, out_ref, solid_ref,
+    assign, corners, solid, residual, stiffness, sems,
+):
+    copies = fetch(
+        [assign_hbm, corners_hbm, solid_hbm, residual_hbm, stiffness_hbm],
+        [assign, corners, solid, residual, stiffness],
+        sems,
+    )
+    for copy in copies:
+        copy.wait()
+    first = 4 * lax.axis_index("sub")
     res = []
     stiff = []
     ones = jnp.ones((1, 768), F32)
     for s in range(4):
-        vertex = jnp.full((1, 768), corners_ref[s, 0].astype(F32), F32)
-        place = jnp.full((1, 768), assign_ref[s].astype(F32), F32)
-        res.append(slot_faces(residual_ref, s, [vertex, place]))
-        stiff.append(slot_faces(stiffness_ref, s, [ones, ones]))
+        vertex = jnp.full((1, 768), corners[s, 0].astype(F32), F32)
+        place = jnp.full((1, 768), assign[first + s].astype(F32), F32)
+        res.append(slot_faces(residual, s, [vertex, place]))
+        stiff.append(slot_faces(stiffness, s, [ones, ones]))
     pairs = [((res, 0), (res, 1)), ((res, 2), (stiff, 0)), ((stiff, 1), (stiff, 2))]
     for at, (one, two) in enumerate(pairs):
         a, b = pair_transpose(stack_rows(*one), stack_rows(*two))
         out_ref[:, 0, at * 256 : at * 256 + 128] = a
         out_ref[:, 0, at * 256 + 128 : at * 256 + 256] = b
+    pieces = []
+    for s in range(4):
+        for p in range(4):
+            pieces += [solid[s, p : p + 1, :].astype(F32), jnp.zeros((1, 2), F32)]
+    solid_ref[...] = jnp.concatenate(pieces, axis=1)
 
 
 def weigh_kernel(in_ref, out_ref, weight_ref, weight_partner_ref, place_ref, slot_ref, vertex_ref):
@@ -163,55 +190,65 @@
     return (lane // 32 == index // 6) & (lane % 8 == index % 6)
 
 
-def solve_kernel(group, in_ref, solid_ref, inverses_ref, basis_ref, local_ref, message_ref, rhs, total):
-    step = pl.program_id(0)
+GROUP = 2
+CHUNKS = 24 // GROUP
+
+
+def solve_kernel(
+    in_ref, solid_ref, inverses_hbm, basis_hbm, local_ref, message_ref,
+    inverses, basis, rhs, sems,
+):
+    size = GROUP * 192
+    chunks = [pl.ds(at * size, size) for at in range(CHUNKS)]
+    copies = fetch(
+        [inverses_hbm.at[chunk] for chunk in chunks] + [basis_hbm],
+        [inverses.at[chunk] for chunk in chunks] + [basis],
+        sems,
+    )
     tiles = [in_ref[:, 0, k * 128 : k * 128 + 128] for k in range(3)]
-
-    @pl.when(step == 0)
-    def _():
-        patch = iota((64, 128), 1) // 8 % 4
-        for k in range(3):
-            value = tiles[k] * solid_ref[...]
-            for p in range(4):
-                row = p * 192 + k * 64
-                rhs[row : row + 64, :] = jnp.where(patch == p, value, 0.0).astype(BF16)
-        total[...] = jnp.zeros_like(total)
-
-    product = jnp.dot(inverses_ref[...], rhs[...], preferred_element_type=F32)
-    held = total[...]
-    for at in range(group):
-        mask = face_mask((192, 128), step * group + at)
-        held = jnp.where(mask, product[at * 192 : at * 192 + 192], held)
-    total[...] = held
-
-    @pl.when(step == pl.num_programs(0) - 1)
-    def _():
-        coarse = jnp.dot(basis_ref[...], rhs[...], preferred_element_type=F32)
-        parts = []
-        for s in range(4):
-            part = jnp.zeros((24, 128), F32)
-            for f in range(6):
-                at = s * 6 + f
-                part = part + jnp.where(
-                    face_mask((24, 128), at), coarse[at * 24 : at * 24 + 24], 0.0
-                )
-            parts += [part, jnp.zeros((8, 128), F32)]
-        row = jnp.sum(jnp.concatenate(parts, axis=0).T, axis=0, keepdims=True)
-        product_sum = jnp.zeros((64, 128), F32)
-        for k in range(3):
-            product_sum = product_sum + tiles[k] * held[k * 64 : k * 64 + 64]
-        inner = jnp.sum(
-            jnp.sum(product_sum, axis=0, keepdims=True) * solid_ref[...], axis=1, keepdims=True
+    patch = iota((64, 128), 1) // 8 % 4
+    for k in range(3):
+        value = tiles[k] * solid_ref[...]
+        for p in range(4):
+            row = p * 192 + k * 64
+            rhs[row : row + 64, :] = jnp.where(patch == p, value, 0.0).astype(BF16)
+    held = jnp.zeros((192, 128), F32)
+    for chunk in range(CHUNKS):
+        copies[chunk].wait()
+        product = jnp.dot(
+            inverses[chunk * size : chunk * size + size, :], rhs[...], preferred_element_type=F32
         )
-        row = jnp.where(iota((1, 128), 1) == 24, inner, row)
-        message_ref[...] = jnp.broadcast_to(row.reshape(1, 1, 128), message_ref.shape)
-        local_ref[...] = held
+        for at in range(GROUP):
+            mask = face_mask((192, 128), chunk * GROUP + at)
+            held = jnp.where(mask, product[at * 192 : at * 192 + 192], held)
+    local_ref[...] = held
+    copies[CHUNKS].wait()
+    coarse = jnp.dot(basis[...], rhs[...], preferred_element_type=F32)
+    parts = []
+    for s in range(4):
+        part = jnp.zeros((24, 128), F32)
+        for f in range(6):
+            at = s * 6 + f
+            part = part + jnp.where(face_mask((24, 128), at), coarse[at * 24 : at * 24 + 24], 0.0)
+        parts += [part, jnp.zeros((8, 128), F32)]
+    row = jnp.sum(jnp.concatenate(parts, axis=0).T, axis=0, keepdims=True)
+    product_sum = jnp.zeros((64, 128), F32)
+    for k in range(3):
+        product_sum = product_sum + tiles[k] * held[k * 64 : k * 64 + 64]
+    inner = jnp.sum(
+        jnp.sum(product_sum, axis=0, keepdims=True) * solid_ref[...], axis=1, keepdims=True
+    )
+    row = jnp.where(iota((1, 128), 1) == 24, inner, row)
+    message_ref[...] = jnp.broadcast_to(row.reshape(1, 1, 128), message_ref.shape)
 
 
 def coarse_kernel(
-    corners_ref, in_ref, place_ref, vertex_ref, inverse_ref, basis_ref, local_ref, solid_ref,
-    out_ref, inner_ref,
+    in_ref, place_ref, vertex_ref, local_ref, solid_ref, one_ref, two_ref, three_ref, own_hbm,
+    corners_hbm, basis_hbm, out_ref, inner_ref, own_ref, corners_ref, basis_ref, columns, sems,
 ):
+    copies = fetch(
+        [own_hbm, corners_hbm, basis_hbm], [own_ref, corners_ref, basis_ref], sems
+    )
     summed = in_ref[0:64, 0, :]
     for y in range(1, 4):
         summed = summed + in_ref[y * 64 : y * 64 + 64, 0, :]
@@ -226,13 +263,25 @@
     by_entry = select_rows(vertex_ref[...], parts)
     own = iota((768, 128), 0) % 3 == iota((768, 128), 1)
     column = jnp.sum(jnp.where(own, by_entry, 0.0), axis=1, keepdims=True)
-    solution = jnp.sum(inverse_ref[...] * column, axis=0, keepdims=True)
+    columns[...] = jnp.broadcast_to(column, (768, 128))
     diagonal = iota((768, 768), 0) == iota((768, 768), 1)
     residual = jnp.sum(jnp.where(diagonal, column, 0.0), axis=0, keepdims=True)
-    rounded = solution.astype(BF16).astype(F32)
+    solution = jnp.zeros((8, 768), F32)
+    copies[0].wait()
+    for ahead, inverse in enumerate((own_ref, one_ref, two_ref, three_ref)):
+        block = lax.rem(lax.axis_index("crs") + ahead, 4) * 192
+        factor = columns[pl.ds(pl.multiple_of(block, 8), 192), :]
+        pieces = []
+        for at in range(6):
+            terms = inverse[:, at * 128 : at * 128 + 128] * factor
+            pieces.append(jnp.sum(terms.reshape(24, 8, 128), axis=0))
+        solution = solution + jnp.concatenate(pieces, axis=1)
+    rounded = jnp.sum(solution, axis=0, keepdims=True).astype(BF16).astype(F32)
     inner_ref[...] = inner + jnp.sum(rounded * residual, axis=1, keepdims=True)
     entry = iota((24, 768), 0)
     lane = iota((24, 768), 1)
+    copies[1].wait()
+    copies[2].wait()
     faces = []
     for s in range(4):
         index = entry % 3
@@ -275,15 +324,26 @@
     return jax.ShapeDtypeStruct(shape, dtype)
 
 
-def call(kernel, inputs, outputs, name):
-    return pl.pallas_call(
+def call(kernel, inputs, outputs, name, scratch=(), megabytes=8):
+    run = pl.pallas_call(
         kernel,
         in_specs=[spec(space) for space in inputs],
         out_specs=tuple(spec() for _ in outputs),
         out_shape=tuple(outputs),
+        scratch_shapes=scratch,
         name=name,
-        compiler_params=pltpu.CompilerParams(vmem_limit_bytes=24 * 2**20),
-    )
+        compiler_params=pltpu.CompilerParams(vmem_limit_bytes=megabytes * 2**20),
+    )
+
+    def placed(*values):
+        return run(
+            *(
+                pltpu.with_memory_space_constraint(value, space) if space is HBM else value
+                for value, space in zip(values, inputs)
+            )
+        )
+
+    return placed
 
 
 def exchange(values, axes):
@@ -291,15 +351,32 @@
 
 
 def body(residual, stiffness, solid, inverses, coarse_basis, assign, corners, coarse_inverse):
-    full_inverse = lax.all_gather(coarse_inverse, "crs", axis=0, tiled=True)
-    mine = lax.dynamic_slice_in_dim(assign, 4 * lax.axis_index("sub"), 4)
-    solid_row = jnp.pad(
-        solid.transpose(0, 2, 1).astype(F32), ((0, 0), (0, 0), (0, 2))
-    ).reshape(1, 128)
+    others = [
+        lax.ppermute(coarse_inverse, "crs", [(y, (y - ahead) % 4) for y in range(4)])
+        for ahead in (1, 2, 3)
+    ]
     basis_rows = coarse_basis.transpose(0, 2, 1, 3).reshape(576, 768)
-
-    (packed,) = call(pack_kernel, [SMEM, SMEM, VMEM, VMEM], [shaped(64, 1, 768)], "pack")(
-        mine, corners, residual.transpose(1, 0, 2), stiffness.transpose(1, 0, 2)
+    dma = pltpu.SemaphoreType.DMA
+
+    packed, solid_row = call(
+        pack_kernel,
+        [HBM] * 5,
+        [shaped(64, 1, 768), shaped(1, 128)],
+        "pack",
+        [
+            SMEM((256,), jnp.int32),
+            SMEM((4, 8), jnp.int32),
+            VMEM((4, 4, 6), jnp.int32),
+            VMEM((6, 4, 768), F32),
+            VMEM((6, 4, 768), F32),
+            dma((5,)),
+        ],
+    )(
+        assign,
+        corners,
+        solid.transpose(0, 2, 1),
+        residual.transpose(1, 0, 2),
+        stiffness.transpose(1, 0, 2),
     )
     weighed, weight, weight_partner, to_place, from_place, to_vertex = call(
         weigh_kernel,
@@ -308,41 +385,41 @@
         + [shaped(n, 256, dtype=BF16) for n in (256, 256, 768)],
         "weigh",
     )(exchange(packed, "sub"))
-
-    group = 4
-    local, message = pl.pallas_call(
-        lambda *refs: solve_kernel(group, *refs),
-        grid=(24 // group,),
-        in_specs=[
-            pl.BlockSpec((64, 1, 384), lambda i: (0, 0, 0)),
-            pl.BlockSpec((1, 128), lambda i: (0, 0)),
-            pl.BlockSpec((group * 192, 768), lambda i: (i, 0)),
-            pl.BlockSpec((576, 768), lambda i: (0, 0)),
+    local, message = call(
+        solve_kernel,
+        [VMEM, VMEM, HBM, HBM],
+        [shaped(192, 128), shaped(256, 1, 128)],
+        "solve",
+        [
+            VMEM((4608, 768), BF16),
+            VMEM((576, 768), BF16),
+            VMEM((768, 128), BF16),
+            dma((CHUNKS + 1,)),
         ],
-        out_specs=(
-            pl.BlockSpec((192, 128), lambda i: (0, 0)),
-            pl.BlockSpec((256, 1, 128), lambda i: (0, 0, 0)),
-        ),
-        out_shape=(shaped(192, 128), shaped(256, 1, 128)),
-        scratch_shapes=[pltpu.VMEM((768, 128), BF16), pltpu.VMEM((192, 128), F32)],
-        name="solve",
-        compiler_params=pltpu.CompilerParams(vmem_limit_bytes=24 * 2**20),
+        16,
     )(exchange(weighed, "sub"), solid_row, inverses.reshape(4608, 768), basis_rows)
-
     solved, inner = call(
         coarse_kernel,
-        [SMEM] + [VMEM] * 7,
+        [VMEM] * 8 + [HBM] * 3,
         [shaped(64, 1, 384), shaped(1, 1)],
         "coarse",
+        [
+            VMEM((192, 768), F32),
+            SMEM((4, 8), jnp.int32),
+            VMEM((576, 768), BF16),
+            VMEM((768, 128), F32),
+            dma((3,)),
+        ],
     )(
-        corners,
         exchange(message, ("crs", "sub")),
         to_place,
         to_vertex,
-        full_inverse,
-        basis_rows,
         local,
         solid_row,
+        *others,
+        coarse_inverse,
+        corners,
+        basis_rows,
     )
     (averaged,) = call(average_kernel, [VMEM] * 5, [shaped(64, 1, 384)], "average")(
         exchange(solved, "sub"), to_place, from_place, weight, weight_partner

time: 123 us -> 105 us (0.85)
  blocking collectives: 72.2 us -> 44.4 us
  starting transfers between devices: 5.73 us -> 23.9 us
  between operations: 14.1 us -> 0.71 us
  waiting for transfers between devices: 10 us -> 19.9 us
  local copies, waits for them, and re-layouts: 9.15 us -> 0 us
  Pallas kernels: 10.8 us -> 15.7 us
    all_to_all x4 -> x3, blocking collectives: 72.2 us -> 44.4 us  [exchange(): return lax.all_to_all(values, axes, 0, 0)]
    all_to_all x1 -> x2, starting transfers between devices: 5.7 us -> 20 us  [exchange(): return lax.all_to_all(values, axes, 0, 0)]
    all_to_all x1 -> x2, waiting for transfers between devices: 9.36 us -> 19.9 us  [exchange(): return lax.all_to_all(values, axes, 0, 0)]
    unnamed x16 -> x0, local copies, waits for them, and re-layouts: 8.3 us -> none
    pallas_call x6, Pallas kernels: 10.8 us -> 15.7 us  [placed(): run(*(pltpu.with_memory_space_constraint(value, space) if space is HBM el...]
    ppermute x0 -> x3, starting transfers between devices: none -> 3.85 us  [body(): lax.ppermute(coarse_inverse, 'crs', [(y, (y - ahead) % 4) for y in range(...]
  transfers between devices with their start and end apart: 2 -> 5, of which waited for: 1 -> 2; matrix products, arithmetic and copies ran while one was open for 1% -> 0% of each run, Pallas kernels for 5% -> 9%
where the time goes in v2:
time: 105 us
  blocking collectives  44.4 us (42%)
  starting transfers between devices  23.9 us (23%)
  waiting for transfers between devices  19.9 us (19%)
  Pallas kernels  15.7 us (15%)
    all_to_all x3, blocking collectives, exchange(): return lax.all_to_all(values, axes, 0, 0)  44.4 us
    all_to_all x2, starting transfers between devices, exchange(): return lax.all_to_all(values, axes, 0, 0)  20 us
    all_to_all x2, waiting for transfers between devices, exchange(): return lax.all_to_all(values, axes, 0, 0)  19.9 us
    pallas_call x6, Pallas kernels, placed(): run(*(pltpu.with_memory_space_constraint(value, space) if space is HBM el...  15.7 us
    ppermute x3, starting transfers between devices, body(): lax.ppermute(coarse_inverse, 'crs', [(y, (y - ahead) % 4) for y in range(...  3.85 us
  transfers between devices with their start and end apart: 5, of which 2 were waited for; matrix products, arithmetic and copies ran while one was open for 0% of the time, Pallas kernels for 9%

profile of v2, /device:TPU:1, one launch (start us, length us, event | category | flops | bytes accessed | tf_op | source)
XLA Modules:
  0.0 104.7 jit_solution(948082285253236212)
XLA Ops:
  0.6 2.0 %pack.1 = (f32[64,1,768]{2,1,0:T(1,128)}, f32[1,128]{1,0:T(1,128)S(1)}) custom-call(s32[256]{0:T(256)} %assign_hbm.1, s32[4,8]{1,0:T(4,128)} %corners_hbm.3, s32[4,4,6]{2,1,0:T(4,128)} %bitcast.15, f32[6,4,768]{2,1,0:T(4,128)} %bitcast.12, f32[6,4,768]{2,1,0:T(4,128)} %bitcast.13), custom_call_target="tpu_custom_call" | custom-call | tf_op jit(solution)/shard_map/pack/pallas_call | solution.py:339
  2.6 13.0 %all-to-all-start = ((f32[64,1,768]{2,1,0:T(1,128)}), f32[64,1,768]{2,1,0:T(1,128)S(1)}, u32[]{:S(2)}, u32[]{:S(2)}) async-start(f32[64,1,768]{2,1,0:T(1,128)} %get-tuple-element.14), calls=%async_computation | async-start | bytes 393216 | tf_op jit(solution)/shard_map/all_to_all | solution.py:350
  15.6 2.8 %collective-permute-start = (f32[192,768]{1,0:T(8,128)}, f32[192,768]{1,0:T(8,128)S(1)}, u32[]{:S(2)}, u32[]{:S(2)}) collective-permute-start(f32[192,768]{1,0:T(8,128)} %own_hbm.1), channel_id=1, source_target_pairs={{0,3},{1,0},{2,1},{3,2},{4,7},{5,4},{6,5},{7,6},{8,11},{9,8},{10,9... | collective-permute-start | bytes 1769480 | tf_op jit(solution)/shard_map/ppermute | solution.py:355
  18.5 0.3 collective-permute-start.1
  18.8 0.7 collective-permute-start.2
  19.5 7.1 %all-to-all-done.in_ref = f32[64,1,768]{2,1,0:T(1,128)S(1)} async-done(((f32[64,1,768]{2,1,0:T(1,128)}), f32[64,1,768]{2,1,0:T(1,128)S(1)}, u32[]{:S(2)}, u32[]{:S(2)}) %all-to-all-start) | async-done | bytes 196640 | tf_op jit(solution)/shard_map/all_to_all | solution.py:350
  26.6 1.3 %weigh.1 = (f32[64,1,384]{2,1,0:T(1,128)S(1)}, f32[256,128]{1,0:T(8,128)S(1)}, f32[256,128]{1,0:T(8,128)S(1)}, bf16[256,256]{1,0:T(8,128)(2,1)S(1)}, bf16[256,25...) custom-call(f32[64,1,768]{2,1,0:T(1,128)S(1)} %all-to-all-done.in_ref), custom_call_target="tpu_custom_call" | custom-call | tf_op jit(solution)/shard_map/weigh/pallas_call | solution.py:339
  27.8 15.7 %all_to_all.25.in_ref = f32[64,1,384]{2,1,0:T(1,128)S(1)} all-to-all(f32[64,1,384]{2,1,0:T(1,128)S(1)} %get-tuple-element.15), channel_id=1, replica_groups=mesh['sub'=64,'crs'=4] {'sub'}, dimensions={0} | all-to-all | bytes 196608 | tf_op jit(solution)/shard_map/all_to_all | solution.py:350
  43.5 7.8 %solve.1 = (f32[192,128]{1,0:T(8,128)S(1)}, f32[256,1,128]{2,1,0:T(1,128)}) custom-call(f32[64,1,384]{2,1,0:T(1,128)S(1)} %all_to_all.25.in_ref, f32[1,128]{1,0:T(1,128)S(1)} %get-tuple-element.16.solid_ref, bf16[4608,768]{1,0:T(8,128)(2,1)} %bitcast.9, bf16[576,768]{1,0:T(8,128)(2,1)} %bitcast.10), custom_call_target="tpu_custom_call" | custom-call | tf_op jit(solution)/shard_map/solve/pallas_call | solution.py:339
  51.3 7.0 %all-to-all-start.2 = ((f32[256,1,128]{2,1,0:T(1,128)}), f32[256,1,128]{2,1,0:T(1,128)S(1)}, u32[]{:S(2)}, u32[]{:S(2)}) async-start(f32[256,1,128]{2,1,0:T(1,128)} %get-tuple-element.17), calls=%async_computation.2 | async-start | bytes 262144 | tf_op jit(solution)/shard_map/all_to_all | solution.py:350
  58.4 0.0 collective-permute-done.one_ref
  58.4 0.0 collective-permute-done.1.two_ref
  58.4 0.0 collective-permute-done.2.three_ref
  58.4 12.8 %all-to-all-done.2.in_ref = f32[256,1,128]{2,1,0:T(1,128)S(1)} async-done(((f32[256,1,128]{2,1,0:T(1,128)}), f32[256,1,128]{2,1,0:T(1,128)S(1)}, u32[]{:S(2)}, u32[]{:S(2)}) %all-to-all-start.2) | async-done | bytes 131104 | tf_op jit(solution)/shard_map/all_to_all | solution.py:350
  71.2 3.0 %coarse.1 = (f32[64,1,384]{2,1,0:T(1,128)S(1)}, f32[1,1]{1,0:T(1,128)}) custom-call(f32[256,1,128]{2,1,0:T(1,128)S(1)} %all-to-all-done.2.in_ref, bf16[256,256]{1,0:T(8,128)(2,1)S(1)} %get-tuple-element.18.place_ref, bf16[768,256]{1,0:T(8,128)(2,1)S(1)} %get-tuple-element.19.vertex_ref, f32[192,128]{1,0:T(8,128)S(1)} %get-tuple-element.20.local_ref, ...), custom_call_target="tpu_custom_call" | custom-call | tf_op jit(solution)/shard_map/coarse/pallas_call | solution.py:339
  74.3 14.4 %all_to_all.26.in_ref = f32[64,1,384]{2,1,0:T(1,128)S(1)} all-to-all(f32[64,1,384]{2,1,0:T(1,128)S(1)} %get-tuple-element.21), channel_id=1, replica_groups=mesh['sub'=64,'crs'=4] {'sub'}, dimensions={0} | all-to-all | bytes 196608 | tf_op jit(solution)/shard_map/all_to_all | solution.py:350
  88.7 0.8 average.1
  89.5 14.3 %all_to_all.27.in_ref = f32[64,1,384]{2,1,0:T(1,128)S(1)} all-to-all(f32[64,1,384]{2,1,0:T(1,128)S(1)} %average.1), channel_id=1, replica_groups=mesh['sub'=64,'crs'=4] {'sub'}, dimensions={0} | all-to-all | bytes 196608 | tf_op jit(solution)/shard_map/all_to_all | solution.py:350
  103.8 0.8 unpack.1
Async XLA Ops:
  2.6 23.9 %all-to-all-start = ((f32[64,1,768]{2,1,0:T(1,128)}), f32[64,1,768]{2,1,0:T(1,128)S(1)}, u32[]{:S(2)}, u32[]{:S(2)}) async-start(f32[64,1,768]{2,1,0:T(1,128)} %get-tuple-element.14), calls=%async_computation | async-start | bytes 393216 | tf_op jit(solution)/shard_map/all_to_all | solution.py:350
  15.6 42.7 %collective-permute-start = (f32[192,768]{1,0:T(8,128)}, f32[192,768]{1,0:T(8,128)S(1)}, u32[]{:S(2)}, u32[]{:S(2)}) collective-permute-start(f32[192,768]{1,0:T(8,128)} %own_hbm.1), channel_id=1, source_target_pairs={{0,3},{1,0},{2,1},{3,2},{4,7},{5,4},{6,5},{7,6},{8,11},{9,8},{10,9... | collective-permute-start | bytes 1769480 | tf_op jit(solution)/shard_map/ppermute | solution.py:355
  18.5 39.9 %collective-permute-start.1 = (f32[192,768]{1,0:T(8,128)}, f32[192,768]{1,0:T(8,128)S(1)}, u32[]{:S(2)}, u32[]{:S(2)}) collective-permute-start(f32[192,768]{1,0:T(8,128)} %own_hbm.1), channel_id=1, source_target_pairs={{0,2},{1,3},{2,0},{3,1},{4,6},{5,7},{6,4},{7,5},{8,10},{9,11},{10,... | collective-permute-start | bytes 1769480 | tf_op jit(solution)/shard_map/ppermute | solution.py:355
  18.8 39.6 %collective-permute-start.2 = (f32[192,768]{1,0:T(8,128)}, f32[192,768]{1,0:T(8,128)S(1)}, u32[]{:S(2)}, u32[]{:S(2)}) collective-permute-start(f32[192,768]{1,0:T(8,128)} %own_hbm.1), channel_id=1, source_target_pairs={{0,1},{1,2},{2,3},{3,0},{4,5},{5,6},{6,7},{7,4},{8,9},{9,10},{10,1... | collective-permute-start | bytes 1769480 | tf_op jit(solution)/shard_map/ppermute | solution.py:355
  51.3 19.9 %all-to-all-start.2 = ((f32[256,1,128]{2,1,0:T(1,128)}), f32[256,1,128]{2,1,0:T(1,128)S(1)}, u32[]{:S(2)}, u32[]{:S(2)}) async-start(f32[256,1,128]{2,1,0:T(1,128)} %get-tuple-element.17), calls=%async_computation.2 | async-start | bytes 262144 | tf_op jit(solution)/shard_map/all_to_all | solution.py:350

commit v3 on v2

--- a/solution.py
+++ b/solution.py
@@ -68,14 +68,18 @@
     )
 
 
-def select_rows(onehot, values):
+def split(values):
     high = values.astype(BF16)
     rest = values - high.astype(F32)
     middle = rest.astype(BF16)
-    low = (rest - middle.astype(F32)).astype(BF16)
+    return high, middle, (rest - middle.astype(F32)).astype(BF16)
+
+
+def select_rows(onehot, values):
     width = values.shape[1]
-    parts = jnp.concatenate([high, middle, low], axis=1)
-    out = jnp.dot(onehot, parts, preferred_element_type=F32)
+    out = jnp.dot(
+        onehot, jnp.concatenate(split(values), axis=1), preferred_element_type=F32
+    )
     return (out[:, :width] + out[:, width : 2 * width]) + out[:, 2 * width :]
 
 
@@ -170,8 +174,6 @@
     both = select_rows(to_place, jnp.concatenate([res, stiff], axis=1))
     res = both[:, :128]
     stiff = both[:, 128:]
-    vertex = jnp.broadcast_to(res[:, 6:7], (256, 128)).T[0:1, :]
-    entry_vertex = (iota((768, 1), 0) // 3).astype(F32)
     stiff_partner = partner(stiff)
     total = stiff + stiff_partner
     weight = stiff / total
@@ -182,7 +184,7 @@
     weight_partner_ref[...] = stiff_partner / total
     place_ref[...] = to_place
     slot_ref[...] = from_place
-    vertex_ref[...] = jnp.where(entry_vertex == vertex, 1.0, 0.0).astype(BF16)
+    vertex_ref[...] = res
 
 
 def face_mask(shape, index):
@@ -190,127 +192,151 @@
     return (lane // 32 == index // 6) & (lane % 8 == index % 6)
 
 
-GROUP = 2
-CHUNKS = 24 // GROUP
+STEPS = 2
 
 
 def solve_kernel(
-    in_ref, solid_ref, inverses_hbm, basis_hbm, local_ref, message_ref,
-    inverses, basis, rhs, sems,
+    in_ref, solid_ref, inverses, basis_hbm, local_ref, message_ref, basis, rhs, total, sem
 ):
-    size = GROUP * 192
-    chunks = [pl.ds(at * size, size) for at in range(CHUNKS)]
-    copies = fetch(
-        [inverses_hbm.at[chunk] for chunk in chunks] + [basis_hbm],
-        [inverses.at[chunk] for chunk in chunks] + [basis],
-        sems,
-    )
-    tiles = [in_ref[:, 0, k * 128 : k * 128 + 128] for k in range(3)]
-    patch = iota((64, 128), 1) // 8 % 4
-    for k in range(3):
-        value = tiles[k] * solid_ref[...]
-        for p in range(4):
-            row = p * 192 + k * 64
-            rhs[row : row + 64, :] = jnp.where(patch == p, value, 0.0).astype(BF16)
-    held = jnp.zeros((192, 128), F32)
-    for chunk in range(CHUNKS):
-        copies[chunk].wait()
-        product = jnp.dot(
-            inverses[chunk * size : chunk * size + size, :], rhs[...], preferred_element_type=F32
+    step = pl.program_id(0)
+    faces = 24 // STEPS
+    copy = pltpu.make_async_copy(basis_hbm, basis, sem)
+
+    @pl.when(step == 0)
+    def _():
+        copy.start()
+        patch = iota((64, 128), 1) // 8 % 4
+        for k in range(3):
+            value = in_ref[:, 0, k * 128 : k * 128 + 128] * solid_ref[...]
+            for p in range(4):
+                row = p * 192 + k * 64
+                rhs[row : row + 64, :] = jnp.where(patch == p, value, 0.0).astype(BF16)
+        total[...] = jnp.zeros_like(total)
+
+    product = jnp.dot(inverses[...], rhs[...], preferred_element_type=F32)
+    held = total[...]
+    for at in range(faces):
+        mask = face_mask((192, 128), step * faces + at)
+        held = jnp.where(mask, product[at * 192 : at * 192 + 192], held)
+    total[...] = held
+
+    @pl.when(step == STEPS - 1)
+    def _():
+        copy.wait()
+        coarse = jnp.dot(basis[...], rhs[...], preferred_element_type=F32)
+        parts = []
+        for s in range(4):
+            part = jnp.zeros((24, 128), F32)
+            for f in range(6):
+                at = s * 6 + f
+                part = part + jnp.where(
+                    face_mask((24, 128), at), coarse[at * 24 : at * 24 + 24], 0.0
+                )
+            parts += [part, jnp.zeros((8, 128), F32)]
+        row = jnp.sum(jnp.concatenate(parts, axis=0).T, axis=0, keepdims=True)
+        product_sum = jnp.zeros((64, 128), F32)
+        for k in range(3):
+            product_sum = product_sum + in_ref[:, 0, k * 128 : k * 128 + 128] * (
+                held[k * 64 : k * 64 + 64]
+            )
+        inner = jnp.sum(
+            jnp.sum(product_sum, axis=0, keepdims=True) * solid_ref[...], axis=1, keepdims=True
         )
-        for at in range(GROUP):
-            mask = face_mask((192, 128), chunk * GROUP + at)
-            held = jnp.where(mask, product[at * 192 : at * 192 + 192], held)
-    local_ref[...] = held
-    copies[CHUNKS].wait()
-    coarse = jnp.dot(basis[...], rhs[...], preferred_element_type=F32)
-    parts = []
+        row = jnp.where(iota((1, 128), 1) == 24, inner, row)
+        message_ref[...] = jnp.broadcast_to(row.reshape(1, 1, 128), message_ref.shape)
+        local_ref[...] = held
+
+
+def pick_kernel(
+    after_ref, vertex_ref, one_ref, two_ref, three_ref, own_hbm, corners_hbm, out_ref, own_ref,
+    corners_ref, columns, sems,
+):
+    copies = fetch([own_hbm, corners_hbm], [own_ref, corners_ref], sems)
+    lane = iota((1, 128), 1)
+    index = jnp.full((1, 128), -1, jnp.int32)
+    copies[1].wait()
     for s in range(4):
-        part = jnp.zeros((24, 128), F32)
-        for f in range(6):
-            at = s * 6 + f
-            part = part + jnp.where(face_mask((24, 128), at), coarse[at * 24 : at * 24 + 24], 0.0)
-        parts += [part, jnp.zeros((8, 128), F32)]
-    row = jnp.sum(jnp.concatenate(parts, axis=0).T, axis=0, keepdims=True)
-    product_sum = jnp.zeros((64, 128), F32)
-    for k in range(3):
-        product_sum = product_sum + tiles[k] * held[k * 64 : k * 64 + 64]
-    inner = jnp.sum(
-        jnp.sum(product_sum, axis=0, keepdims=True) * solid_ref[...], axis=1, keepdims=True
-    )
-    row = jnp.where(iota((1, 128), 1) == 24, inner, row)
-    message_ref[...] = jnp.broadcast_to(row.reshape(1, 1, 128), message_ref.shape)
-
-
-def coarse_kernel(
-    in_ref, place_ref, vertex_ref, local_ref, solid_ref, one_ref, two_ref, three_ref, own_hbm,
-    corners_hbm, basis_hbm, out_ref, inner_ref, own_ref, corners_ref, basis_ref, columns, sems,
-):
-    copies = fetch(
-        [own_hbm, corners_hbm, basis_hbm], [own_ref, corners_ref, basis_ref], sems
-    )
-    summed = in_ref[0:64, 0, :]
-    for y in range(1, 4):
-        summed = summed + in_ref[y * 64 : y * 64 + 64, 0, :]
-    inner = jnp.sum(jnp.sum(summed, axis=0, keepdims=True)[:, 24:25], axis=1, keepdims=True)
-    pad = jnp.zeros((64, 96), F32)
-    parts = jnp.concatenate(
-        [jnp.concatenate([summed[:, s * 32 : s * 32 + 32], pad], axis=1) for s in range(4)], axis=0
-    )
-    parts = select_rows(place_ref[...], parts)
-    for direction, count in ((2, 3), (1, 6), (0, 12)):
-        parts = parts + step_back(lanes_ahead(parts, count), direction)
-    by_entry = select_rows(vertex_ref[...], parts)
-    own = iota((768, 128), 0) % 3 == iota((768, 128), 1)
-    column = jnp.sum(jnp.where(own, by_entry, 0.0), axis=1, keepdims=True)
-    columns[...] = jnp.broadcast_to(column, (768, 128))
-    diagonal = iota((768, 768), 0) == iota((768, 768), 1)
-    residual = jnp.sum(jnp.where(diagonal, column, 0.0), axis=0, keepdims=True)
-    solution = jnp.zeros((8, 768), F32)
+        for c in range(8):
+            first = s * 32 + c * 3
+            here = (lane >= first) & (lane < first + 3)
+            index = jnp.where(here, 3 * corners_ref[s, c] + lane - first, index)
+    wanted = jnp.where(iota((768, 128), 0) == index, 1.0, 0.0).astype(BF16)
     copies[0].wait()
     for ahead, inverse in enumerate((own_ref, one_ref, two_ref, three_ref)):
         block = lax.rem(lax.axis_index("crs") + ahead, 4) * 192
-        factor = columns[pl.ds(pl.multiple_of(block, 8), 192), :]
-        pieces = []
-        for at in range(6):
-            terms = inverse[:, at * 128 : at * 128 + 128] * factor
-            pieces.append(jnp.sum(terms.reshape(24, 8, 128), axis=0))
-        solution = solution + jnp.concatenate(pieces, axis=1)
-    rounded = jnp.sum(solution, axis=0, keepdims=True).astype(BF16).astype(F32)
-    inner_ref[...] = inner + jnp.sum(rounded * residual, axis=1, keepdims=True)
-    entry = iota((24, 768), 0)
-    lane = iota((24, 768), 1)
-    copies[1].wait()
-    copies[2].wait()
+        picked = jnp.dot(
+            jnp.concatenate(split(inverse[...]), axis=0), wanted, preferred_element_type=F32
+        )
+        columns[pl.ds(pl.multiple_of(block, 8), 192), :] = (
+            picked[:192] + picked[192:384]
+        ) + picked[384:]
+    vertex = 3.0 * vertex_ref[:, 6:7]
+    entry = iota((256, 768), 1).astype(F32)
+    values = columns[...]
+    for j in range(3):
+        rows = jnp.where(entry == vertex + j, 1.0, 0.0).astype(BF16)
+        out_ref[j * 256 : j * 256 + 256, :] = select_rows(rows, values)
+
+
+def coarse_kernel(
+    in_ref, place_ref, picked_ref, local_ref, solid_ref, basis_hbm, out_ref, basis_ref, sem
+):
+    copy = pltpu.make_async_copy(basis_hbm, basis_ref, sem)
+    copy.start()
+    summed = in_ref[0:64, 0, :]
+    me = lax.axis_index("sub")
+    mine = in_ref[pl.ds(me, 1), 0, :]
+    for y in range(1, 4):
+        summed = summed + in_ref[y * 64 : y * 64 + 64, 0, :]
+        mine = mine + in_ref[pl.ds(y * 64 + me, 1), 0, :]
+    parts = jnp.concatenate([summed[:, s * 32 : s * 32 + 32] for s in range(4)], axis=0)
+    parts = jnp.concatenate(
+        [part.astype(F32) for part in split(parts)] + [jnp.zeros((256, 32), F32)], axis=1
+    )
+    parts = jnp.dot(place_ref[...], parts.astype(BF16), preferred_element_type=F32)
+    parts = (parts + lanes_ahead(parts, 32)) + lanes_ahead(parts, 64)
+    for direction, count in ((2, 3), (1, 6), (0, 12)):
+        parts = parts + step_back(lanes_ahead(parts, count), direction)
+    terms = jnp.zeros((256, 128), F32)
+    for j in range(3):
+        terms = terms + picked_ref[j * 256 : j * 256 + 256, :] * parts[:, j : j + 1]
+    rounded = jnp.sum(terms, axis=0, keepdims=True).astype(BF16).astype(F32)
+    inner = jnp.sum(rounded * mine, axis=1, keepdims=True) + mine[:, 24:25]
+    values = jnp.broadcast_to(rounded, (128, 128)).T
+    copy.wait()
     faces = []
     for s in range(4):
-        index = entry % 3
-        for c in range(8):
-            index = jnp.where(entry // 3 == c, entry % 3 + 3 * corners_ref[s, c], index)
-        values = jnp.sum(jnp.where(lane == index, rounded, 0.0), axis=1, keepdims=True)
         rows = []
         for f in range(6):
-            block = basis_ref[(s * 6 + f) * 24 : (s * 6 + f) * 24 + 24, :].astype(F32)
-            rows.append(jnp.sum(block * values, axis=0, keepdims=True))
+            at = s * 6 + f
+            block = basis_ref[at * 24 : at * 24 + 24, :].astype(F32)
+            factor = values[s * 32 : s * 32 + 24, 0:1]
+            rows.append(jnp.sum(block * factor, axis=0, keepdims=True))
         faces.append(jnp.concatenate(rows + [jnp.zeros((2, 768), F32)], axis=0))
     a, b = pair_transpose(stack_rows(faces, 0), stack_rows(faces, 1))
     c, _ = pair_transpose(stack_rows(faces, 2), jnp.zeros((128, 64), F32))
     for k, tile in enumerate((a, b, c)):
-        out_ref[:, 0, k * 128 : k * 128 + 128] = solid_ref[...] * (
-            local_ref[k * 64 : k * 64 + 64] + tile
-        )
+        tile = solid_ref[...] * (local_ref[k * 64 : k * 64 + 64] + tile)
+        if k == 0:
+            tile = jnp.where(iota((64, 128), 1) == 6, inner, tile)
+        out_ref[:, 0, k * 128 : k * 128 + 128] = tile
 
 
 def average_kernel(in_ref, place_ref, slot_ref, weight_ref, weight_partner_ref, out_ref):
     tiles = [in_ref[:, 0, k * 128 : k * 128 + 128] for k in range(3)]
+    inner = jnp.sum(tiles[0], axis=0, keepdims=True)[:, 6:7]
     values = select_rows(place_ref[...], to_slots(tiles))
     values = weight_ref[...] * values + weight_partner_ref[...] * partner(values)
     back = select_rows(slot_ref[...], values)
     for k in range(3):
-        out_ref[:, 0, k * 128 : k * 128 + 128] = from_slots(back, k)
-
-
-def unpack_kernel(in_ref, out_ref):
+        tile = from_slots(back, k)
+        if k == 0:
+            tile = jnp.where(iota((64, 128), 1) == 6, inner, tile)
+        out_ref[:, 0, k * 128 : k * 128 + 128] = tile
+
+
+def unpack_kernel(in_ref, out_ref, inner_ref):
+    inner_ref[...] = in_ref[0:1, 0, 6:7]
     faces = unpack_faces([in_ref[:, 0, k * 128 : k * 128 + 128] for k in range(3)])
     for f in range(6):
         out_ref[f] = jnp.concatenate([faces[s][f : f + 1, :] for s in range(4)], axis=0)
@@ -378,53 +404,66 @@
         residual.transpose(1, 0, 2),
         stiffness.transpose(1, 0, 2),
     )
-    weighed, weight, weight_partner, to_place, from_place, to_vertex = call(
+    weighed, weight, weight_partner, to_place, from_place, vertex = call(
         weigh_kernel,
         [VMEM],
-        [shaped(64, 1, 384), shaped(256, 128), shaped(256, 128)]
-        + [shaped(n, 256, dtype=BF16) for n in (256, 256, 768)],
+        [
+            shaped(64, 1, 384),
+            shaped(256, 128),
+            shaped(256, 128),
+            shaped(256, 256, dtype=BF16),
+            shaped(256, 256, dtype=BF16),
+            shaped(256, 128),
+        ],
         "weigh",
     )(exchange(packed, "sub"))
-    local, message = call(
+    whole = [pl.BlockSpec(memory_space=VMEM), pl.BlockSpec(memory_space=HBM)]
+    rows = 4608 // STEPS
+    local, message = pl.pallas_call(
         solve_kernel,
-        [VMEM, VMEM, HBM, HBM],
-        [shaped(192, 128), shaped(256, 1, 128)],
-        "solve",
-        [
-            VMEM((4608, 768), BF16),
+        grid=(STEPS,),
+        in_specs=[whole[0], whole[0], pl.BlockSpec((rows, 768), lambda i: (i, 0)), whole[1]],
+        out_specs=(whole[0], whole[0]),
+        out_shape=(shaped(192, 128), shaped(256, 1, 128)),
+        scratch_shapes=[
             VMEM((576, 768), BF16),
             VMEM((768, 128), BF16),
-            dma((CHUNKS + 1,)),
-        ],
-        16,
-    )(exchange(weighed, "sub"), solid_row, inverses.reshape(4608, 768), basis_rows)
-    solved, inner = call(
-        coarse_kernel,
-        [VMEM] * 8 + [HBM] * 3,
-        [shaped(64, 1, 384), shaped(1, 1)],
-        "coarse",
+            VMEM((192, 128), F32),
+            dma(()),
+        ],
+        name="solve",
+        compiler_params=pltpu.CompilerParams(vmem_limit_bytes=16 * 2**20),
+    )(
+        exchange(weighed, "sub"),
+        solid_row,
+        pltpu.with_memory_space_constraint(inverses.reshape(4608, 768), HBM),
+        pltpu.with_memory_space_constraint(basis_rows, HBM),
+    )
+    (picked,) = call(
+        pick_kernel,
+        [VMEM] * 5 + [HBM] * 2,
+        [shaped(768, 128)],
+        "pick",
         [
             VMEM((192, 768), F32),
             SMEM((4, 8), jnp.int32),
-            VMEM((576, 768), BF16),
             VMEM((768, 128), F32),
-            dma((3,)),
-        ],
-    )(
-        exchange(message, ("crs", "sub")),
-        to_place,
-        to_vertex,
-        local,
-        solid_row,
-        *others,
-        coarse_inverse,
-        corners,
-        basis_rows,
-    )
+            dma((2,)),
+        ],
+    )(local, vertex, *others, coarse_inverse, corners)
+    (solved,) = call(
+        coarse_kernel,
+        [VMEM] * 5 + [HBM],
+        [shaped(64, 1, 384)],
+        "coarse",
+        [VMEM((576, 768), BF16), dma(())],
+    )(exchange(message, ("crs", "sub")), to_place, picked, local, solid_row, basis_rows)
     (averaged,) = call(average_kernel, [VMEM] * 5, [shaped(64, 1, 384)], "average")(
         exchange(solved, "sub"), to_place, from_place, weight, weight_partner
     )
-    (out,) = call(unpack_kernel, [VMEM], [shaped(6, 4, 768)], "unpack")(exchange(averaged, "sub"))
+    out, inner = call(unpack_kernel, [VMEM], [shaped(6, 4, 768), shaped(1, 1)], "unpack")(
+        exchange(averaged, "sub")
+    )
     return out.transpose(1, 0, 2), inner.reshape(1)
 
 

time: 105 us -> 102 us (0.971)
  waiting for transfers between devices: 19.9 us -> 16.3 us
    pallas_call x6, Pallas kernels: 15.7 us -> 10.2 us  [placed(): run(*(pltpu.with_memory_space_constraint(value, space) if space is HBM el...]
    pallas_call x0 -> x1, Pallas kernels: none -> 5.47 us  [body(): pl.pallas_call(solve_kernel, grid=(STEPS,), in_specs=[whole[0], whole[0],...]
    all_to_all x2, waiting for transfers between devices: 19.9 us -> 16.3 us  [exchange(): return lax.all_to_all(values, axes, 0, 0)]
where the time goes in v3:
time: 102 us
  blocking collectives  44.4 us (44%)
  starting transfers between devices  24.5 us (24%)
  waiting for transfers between devices  16.3 us (16%)
  Pallas kernels  15.7 us (15%)
    all_to_all x3, blocking collectives, exchange(): return lax.all_to_all(values, axes, 0, 0)  44.4 us
    all_to_all x2, starting transfers between devices, exchange(): return lax.all_to_all(values, axes, 0, 0)  20 us
    all_to_all x2, waiting for transfers between devices, exchange(): return lax.all_to_all(values, axes, 0, 0)  16.3 us
    pallas_call x6, Pallas kernels, placed(): run(*(pltpu.with_memory_space_constraint(value, space) if space is HBM el...  10.2 us
    pallas_call x1, Pallas kernels, body(): pl.pallas_call(solve_kernel, grid=(STEPS,), in_specs=[whole[0], whole[0],...  5.47 us
    ppermute x3, starting transfers between devices, body(): lax.ppermute(coarse_inverse, 'crs', [(y, (y - ahead) % 4) for y in range(...  4.47 us
  transfers between devices with their start and end apart: 5, of which 2 were waited for; matrix products, arithmetic and copies ran while one was open for 0% of the time, Pallas kernels for 9%

profile of v3, /device:TPU:1, one launch (start us, length us, event | category | flops | bytes accessed | tf_op | source)
XLA Modules:
  0.0 101.7 jit_solution(17003432574044181191)
XLA Ops:
  0.6 2.0 %pack.1 = (f32[64,1,768]{2,1,0:T(1,128)}, f32[1,128]{1,0:T(1,128)S(1)}) custom-call(s32[256]{0:T(256)} %assign_hbm.1, s32[4,8]{1,0:T(4,128)} %corners_hbm.3, s32[4,4,6]{2,1,0:T(4,128)} %bitcast.14, f32[6,4,768]{2,1,0:T(4,128)} %bitcast.12, f32[6,4,768]{2,1,0:T(4,128)} %bitcast.13), custom_call_target="tpu_custom_call" | custom-call | tf_op jit(solution)/shard_map/pack/pallas_call | solution.py:365
  2.6 13.0 %all-to-all-start = ((f32[64,1,768]{2,1,0:T(1,128)}), f32[64,1,768]{2,1,0:T(1,128)S(1)}, u32[]{:S(2)}, u32[]{:S(2)}) async-start(f32[64,1,768]{2,1,0:T(1,128)} %get-tuple-element.14), calls=%async_computation | async-start | bytes 393216 | tf_op jit(solution)/shard_map/all_to_all | solution.py:376
  15.6 3.0 %collective-permute-start.1 = (f32[192,768]{1,0:T(8,128)}, f32[192,768]{1,0:T(8,128)S(1)}, u32[]{:S(2)}, u32[]{:S(2)}) collective-permute-start(f32[192,768]{1,0:T(8,128)} %own_hbm.1), channel_id=1, source_target_pairs={{0,2},{1,3},{2,0},{3,1},{4,6},{5,7},{6,4},{7,5},{8,10},{9,11},{10,... | collective-permute-start | bytes 1769480 | tf_op jit(solution)/shard_map/ppermute | solution.py:381
  18.6 0.8 collective-permute-start
  19.4 0.7 collective-permute-start.2
  20.1 6.5 %all-to-all-done.in_ref = f32[64,1,768]{2,1,0:T(1,128)S(1)} async-done(((f32[64,1,768]{2,1,0:T(1,128)}), f32[64,1,768]{2,1,0:T(1,128)S(1)}, u32[]{:S(2)}, u32[]{:S(2)}) %all-to-all-start) | async-done | bytes 196640 | tf_op jit(solution)/shard_map/all_to_all | solution.py:376
  26.6 1.2 %weigh.1 = (f32[64,1,384]{2,1,0:T(1,128)S(1)}, f32[256,128]{1,0:T(8,128)S(1)}, f32[256,128]{1,0:T(8,128)S(1)}, bf16[256,256]{1,0:T(8,128)(2,1)S(1)}, bf16[256,25...) custom-call(f32[64,1,768]{2,1,0:T(1,128)S(1)} %all-to-all-done.in_ref), custom_call_target="tpu_custom_call" | custom-call | tf_op jit(solution)/shard_map/weigh/pallas_call | solution.py:365
  27.8 15.7 %all_to_all.25.in_ref = f32[64,1,384]{2,1,0:T(1,128)S(1)} all-to-all(f32[64,1,384]{2,1,0:T(1,128)S(1)} %get-tuple-element.15), channel_id=1, replica_groups=mesh['sub'=64,'crs'=4] {'sub'}, dimensions={0} | all-to-all | bytes 196608 | tf_op jit(solution)/shard_map/all_to_all | solution.py:376
  43.5 5.5 %solve.1 = (f32[192,128]{1,0:T(8,128)S(1)}, f32[256,1,128]{2,1,0:T(1,128)}) custom-call(f32[64,1,384]{2,1,0:T(1,128)S(1)} %all_to_all.25.in_ref, f32[1,128]{1,0:T(1,128)S(1)} %get-tuple-element.16.solid_ref, bf16[4608,768]{1,0:T(8,128)(2,1)} %bitcast.9, bf16[576,768]{1,0:T(8,128)(2,1)} %bitcast.10), custom_call_target="tpu_custom_call" | custom-call | tf_op jit(solution)/shard_map/solve/pallas_call | solution.py:422
  48.9 7.0 %all-to-all-start.2 = ((f32[256,1,128]{2,1,0:T(1,128)}), f32[256,1,128]{2,1,0:T(1,128)S(1)}, u32[]{:S(2)}, u32[]{:S(2)}) async-start(f32[256,1,128]{2,1,0:T(1,128)} %get-tuple-element.17), calls=%async_computation.2 | async-start | bytes 262144 | tf_op jit(solution)/shard_map/all_to_all | solution.py:376
  56.0 0.0 collective-permute-done.1.two_ref
  56.0 0.0 collective-permute-done.one_ref
  56.0 0.0 collective-permute-done.2.three_ref
  56.0 3.0 %pick.1.picked_ref = f32[768,128]{1,0:T(8,128)S(1)} custom-call(f32[192,128]{1,0:T(8,128)S(1)} %get-tuple-element.19.after_ref.local_ref, f32[256,128]{1,0:T(8,128)S(1)} %get-tuple-element.20.vertex_ref, f32[192,768]{1,0:T(8,128)S(1)} %collective-permute-done.one_ref, f32[192,768]{1,0:T(8,128)S(1)} %collective-permute-done.1.two_ref, ...), custom_call_target="tpu_custom_call" | custom-call | tf_op jit(solution)/shard_map/pick/pallas_call | solution.py:365
  59.0 9.9 %all-to-all-done.2.in_ref = f32[256,1,128]{2,1,0:T(1,128)S(1)} async-done(((f32[256,1,128]{2,1,0:T(1,128)}), f32[256,1,128]{2,1,0:T(1,128)S(1)}, u32[]{:S(2)}, u32[]{:S(2)}) %all-to-all-start.2) | async-done | bytes 131104 | tf_op jit(solution)/shard_map/all_to_all | solution.py:376
  68.9 2.4 %coarse.1 = f32[64,1,384]{2,1,0:T(1,128)S(1)} custom-call(f32[256,1,128]{2,1,0:T(1,128)S(1)} %all-to-all-done.2.in_ref, bf16[256,256]{1,0:T(8,128)(2,1)S(1)} %get-tuple-element.18.place_ref, f32[768,128]{1,0:T(8,128)S(1)} %pick.1.picked_ref, f32[192,128]{1,0:T(8,128)S(1)} %get-tuple-element.19.after_ref.local_ref, f32[1,128]{1,0:T(1,128)S(1)} %get-tuple-element.16.solid_ref, ...), custom_call_target="tpu_custom_call" | custom-call | tf_op jit(solution)/shard_map/coarse/pallas_call | solution.py:365
  71.3 14.4 %all_to_all.26.in_ref = f32[64,1,384]{2,1,0:T(1,128)S(1)} all-to-all(f32[64,1,384]{2,1,0:T(1,128)S(1)} %coarse.1), channel_id=1, replica_groups=mesh['sub'=64,'crs'=4] {'sub'}, dimensions={0} | all-to-all | bytes 196608 | tf_op jit(solution)/shard_map/all_to_all | solution.py:376
  85.7 0.8 average.1
  86.5 14.3 %all_to_all.27.in_ref = f32[64,1,384]{2,1,0:T(1,128)S(1)} all-to-all(f32[64,1,384]{2,1,0:T(1,128)S(1)} %average.1), channel_id=1, replica_groups=mesh['sub'=64,'crs'=4] {'sub'}, dimensions={0} | all-to-all | bytes 196608 | tf_op jit(solution)/shard_map/all_to_all | solution.py:376
  100.8 0.8 unpack.1
Async XLA Ops:
  2.6 23.9 %all-to-all-start = ((f32[64,1,768]{2,1,0:T(1,128)}), f32[64,1,768]{2,1,0:T(1,128)S(1)}, u32[]{:S(2)}, u32[]{:S(2)}) async-start(f32[64,1,768]{2,1,0:T(1,128)} %get-tuple-element.14), calls=%async_computation | async-start | bytes 393216 | tf_op jit(solution)/shard_map/all_to_all | solution.py:376
  15.6 40.3 %collective-permute-start.1 = (f32[192,768]{1,0:T(8,128)}, f32[192,768]{1,0:T(8,128)S(1)}, u32[]{:S(2)}, u32[]{:S(2)}) collective-permute-start(f32[192,768]{1,0:T(8,128)} %own_hbm.1), channel_id=1, source_target_pairs={{0,2},{1,3},{2,0},{3,1},{4,6},{5,7},{6,4},{7,5},{8,10},{9,11},{10,... | collective-permute-start | bytes 1769480 | tf_op jit(solution)/shard_map/ppermute | solution.py:381
  18.6 37.4 %collective-permute-start = (f32[192,768]{1,0:T(8,128)}, f32[192,768]{1,0:T(8,128)S(1)}, u32[]{:S(2)}, u32[]{:S(2)}) collective-permute-start(f32[192,768]{1,0:T(8,128)} %own_hbm.1), channel_id=1, source_target_pairs={{0,3},{1,0},{2,1},{3,2},{4,7},{5,4},{6,5},{7,6},{8,11},{9,8},{10,9... | collective-permute-start | bytes 1769480 | tf_op jit(solution)/shard_map/ppermute | solution.py:381
  19.4 36.6 %collective-permute-start.2 = (f32[192,768]{1,0:T(8,128)}, f32[192,768]{1,0:T(8,128)S(1)}, u32[]{:S(2)}, u32[]{:S(2)}) collective-permute-start(f32[192,768]{1,0:T(8,128)} %own_hbm.1), channel_id=1, source_target_pairs={{0,1},{1,2},{2,3},{3,0},{4,5},{5,6},{6,7},{7,4},{8,9},{9,10},{10,1... | collective-permute-start | bytes 1769480 | tf_op jit(solution)/shard_map/ppermute | solution.py:381
  48.9 19.9 %all-to-all-start.2 = ((f32[256,1,128]{2,1,0:T(1,128)}), f32[256,1,128]{2,1,0:T(1,128)S(1)}, u32[]{:S(2)}, u32[]{:S(2)}) async-start(f32[256,1,128]{2,1,0:T(1,128)} %get-tuple-element.17), calls=%async_computation.2 | async-start | bytes 262144 | tf_op jit(solution)/shard_map/all_to_all | solution.py:376

commit v4 on v3

--- a/solution.py
+++ b/solution.py
@@ -163,7 +163,7 @@
     solid_ref[...] = jnp.concatenate(pieces, axis=1)
 
 
-def weigh_kernel(in_ref, out_ref, weight_ref, weight_partner_ref, place_ref, slot_ref, vertex_ref):
+def weigh_kernel(in_ref, out_ref, weight_ref, place_ref, slot_ref, vertex_ref):
     tiles = [in_ref[:, 0, at * 128 : at * 128 + 128] for at in range(6)]
     res = to_slots(tiles[:3])
     stiff = to_slots(tiles[3:])
@@ -174,17 +174,14 @@
     both = select_rows(to_place, jnp.concatenate([res, stiff], axis=1))
     res = both[:, :128]
     stiff = both[:, 128:]
-    stiff_partner = partner(stiff)
-    total = stiff + stiff_partner
-    weight = stiff / total
+    weight = stiff / (stiff + partner(stiff))
     back = select_rows(from_place, weight * (res + partner(res)))
     for k in range(3):
         out_ref[:, 0, k * 128 : k * 128 + 128] = from_slots(back, k)
     weight_ref[...] = weight
-    weight_partner_ref[...] = stiff_partner / total
     place_ref[...] = to_place
     slot_ref[...] = from_place
-    vertex_ref[...] = res
+    vertex_ref[...] = jnp.broadcast_to(res[:, 6:7], (256, 128)).T[0:1]
 
 
 def face_mask(shape, index):
@@ -192,48 +189,45 @@
     return (lane // 32 == index // 6) & (lane % 8 == index % 6)
 
 
+def parts_kernel(in_ref, solid_ref, basis, message_ref, rhs):
+    patch = iota((64, 128), 1) // 8 % 4
+    for k in range(3):
+        value = in_ref[:, 0, k * 128 : k * 128 + 128] * solid_ref[...]
+        for p in range(4):
+            row = p * 192 + k * 64
+            rhs[row : row + 64, :] = jnp.where(patch == p, value, 0.0).astype(BF16)
+    coarse = jnp.dot(basis[...], rhs[...], preferred_element_type=F32)
+    parts = []
+    for s in range(4):
+        part = jnp.zeros((24, 128), F32)
+        for f in range(6):
+            at = s * 6 + f
+            part = part + jnp.where(face_mask((24, 128), at), coarse[at * 24 : at * 24 + 24], 0.0)
+        parts += [part, jnp.zeros((8, 128), F32)]
+    row = jnp.sum(jnp.concatenate(parts, axis=0).T, axis=0, keepdims=True)
+    message_ref[...] = jnp.broadcast_to(row.reshape(1, 1, 128), message_ref.shape)
+
+
 STEPS = 2
 
 
-def solve_kernel(
-    in_ref, solid_ref, inverses, basis_hbm, local_ref, message_ref, basis, rhs, total, sem
-):
+def solve_kernel(in_ref, solid_ref, rhs, inverses, local_ref, inner_ref):
     step = pl.program_id(0)
     faces = 24 // STEPS
-    copy = pltpu.make_async_copy(basis_hbm, basis, sem)
 
     @pl.when(step == 0)
     def _():
-        copy.start()
-        patch = iota((64, 128), 1) // 8 % 4
-        for k in range(3):
-            value = in_ref[:, 0, k * 128 : k * 128 + 128] * solid_ref[...]
-            for p in range(4):
-                row = p * 192 + k * 64
-                rhs[row : row + 64, :] = jnp.where(patch == p, value, 0.0).astype(BF16)
-        total[...] = jnp.zeros_like(total)
+        local_ref[...] = jnp.zeros_like(local_ref)
 
     product = jnp.dot(inverses[...], rhs[...], preferred_element_type=F32)
-    held = total[...]
+    held = local_ref[...]
     for at in range(faces):
         mask = face_mask((192, 128), step * faces + at)
         held = jnp.where(mask, product[at * 192 : at * 192 + 192], held)
-    total[...] = held
+    local_ref[...] = held
 
     @pl.when(step == STEPS - 1)
     def _():
-        copy.wait()
-        coarse = jnp.dot(basis[...], rhs[...], preferred_element_type=F32)
-        parts = []
-        for s in range(4):
-            part = jnp.zeros((24, 128), F32)
-            for f in range(6):
-                at = s * 6 + f
-                part = part + jnp.where(
-                    face_mask((24, 128), at), coarse[at * 24 : at * 24 + 24], 0.0
-                )
-            parts += [part, jnp.zeros((8, 128), F32)]
-        row = jnp.sum(jnp.concatenate(parts, axis=0).T, axis=0, keepdims=True)
         product_sum = jnp.zeros((64, 128), F32)
         for k in range(3):
             product_sum = product_sum + in_ref[:, 0, k * 128 : k * 128 + 128] * (
@@ -242,16 +236,15 @@
         inner = jnp.sum(
             jnp.sum(product_sum, axis=0, keepdims=True) * solid_ref[...], axis=1, keepdims=True
         )
-        row = jnp.where(iota((1, 128), 1) == 24, inner, row)
-        message_ref[...] = jnp.broadcast_to(row.reshape(1, 1, 128), message_ref.shape)
-        local_ref[...] = held
-
-
-def pick_kernel(
-    after_ref, vertex_ref, one_ref, two_ref, three_ref, own_hbm, corners_hbm, out_ref, own_ref,
-    corners_ref, columns, sems,
+        inner_ref[...] = jnp.broadcast_to(inner, (1, 128))
+
+
+def columns_kernel(
+    after_ref, inverse_hbm, corners_hbm, basis_hbm, out_ref, basis_ref, inverse, corners, sems
 ):
-    copies = fetch([own_hbm, corners_hbm], [own_ref, corners_ref], sems)
+    copies = fetch(
+        [inverse_hbm, corners_hbm, basis_hbm], [inverse, corners, basis_ref], sems
+    )
     lane = iota((1, 128), 1)
     index = jnp.full((1, 128), -1, jnp.int32)
     copies[1].wait()
@@ -259,30 +252,32 @@
         for c in range(8):
             first = s * 32 + c * 3
             here = (lane >= first) & (lane < first + 3)
-            index = jnp.where(here, 3 * corners_ref[s, c] + lane - first, index)
+            index = jnp.where(here, 3 * corners[s, c] + lane - first, index)
     wanted = jnp.where(iota((768, 128), 0) == index, 1.0, 0.0).astype(BF16)
     copies[0].wait()
-    for ahead, inverse in enumerate((own_ref, one_ref, two_ref, three_ref)):
+    picked = jnp.dot(
+        jnp.concatenate(split(inverse[...]), axis=0), wanted, preferred_element_type=F32
+    )
+    out_ref[...] = jnp.concatenate([picked[:192], picked[192:384], picked[384:]], axis=1)
+    copies[2].wait()
+
+
+def pick_kernel(after_ref, vertex_ref, own_ref, one_ref, two_ref, three_ref, out_ref, columns):
+    for ahead, block_ref in enumerate((own_ref, one_ref, two_ref, three_ref)):
         block = lax.rem(lax.axis_index("crs") + ahead, 4) * 192
-        picked = jnp.dot(
-            jnp.concatenate(split(inverse[...]), axis=0), wanted, preferred_element_type=F32
-        )
-        columns[pl.ds(pl.multiple_of(block, 8), 192), :] = (
-            picked[:192] + picked[192:384]
-        ) + picked[384:]
-    vertex = 3.0 * vertex_ref[:, 6:7]
+        columns[pl.ds(pl.multiple_of(block, 8), 192), :] = block_ref[...]
+    parts = columns[...].astype(BF16)
+    vertex = 3.0 * jnp.broadcast_to(vertex_ref[...], (128, 256)).T[:, 0:1]
     entry = iota((256, 768), 1).astype(F32)
-    values = columns[...]
     for j in range(3):
         rows = jnp.where(entry == vertex + j, 1.0, 0.0).astype(BF16)
-        out_ref[j * 256 : j * 256 + 256, :] = select_rows(rows, values)
+        out = jnp.dot(rows, parts, preferred_element_type=F32)
+        out_ref[j * 256 : j * 256 + 256, :] = (out[:, :128] + out[:, 128:256]) + out[:, 256:]
 
 
 def coarse_kernel(
-    in_ref, place_ref, picked_ref, local_ref, solid_ref, basis_hbm, out_ref, basis_ref, sem
+    in_ref, place_ref, picked_ref, local_ref, inner_ref, near_ref, solid_ref, basis_ref, out_ref
 ):
-    copy = pltpu.make_async_copy(basis_hbm, basis_ref, sem)
-    copy.start()
     summed = in_ref[0:64, 0, :]
     me = lax.axis_index("sub")
     mine = in_ref[pl.ds(me, 1), 0, :]
@@ -301,9 +296,9 @@
     for j in range(3):
         terms = terms + picked_ref[j * 256 : j * 256 + 256, :] * parts[:, j : j + 1]
     rounded = jnp.sum(terms, axis=0, keepdims=True).astype(BF16).astype(F32)
-    inner = jnp.sum(rounded * mine, axis=1, keepdims=True) + mine[:, 24:25]
+    inner = jnp.sum(rounded * mine, axis=1, keepdims=True)
+    inner = (inner_ref[...] + near_ref[...]) + 0.5 * inner
     values = jnp.broadcast_to(rounded, (128, 128)).T
-    copy.wait()
     faces = []
     for s in range(4):
         rows = []
@@ -322,21 +317,19 @@
         out_ref[:, 0, k * 128 : k * 128 + 128] = tile
 
 
-def average_kernel(in_ref, place_ref, slot_ref, weight_ref, weight_partner_ref, out_ref):
+def average_kernel(in_ref, place_ref, slot_ref, weight_ref, out_ref, inner_ref):
     tiles = [in_ref[:, 0, k * 128 : k * 128 + 128] for k in range(3)]
-    inner = jnp.sum(tiles[0], axis=0, keepdims=True)[:, 6:7]
+    inner_ref[...] = jnp.sum(tiles[0], axis=0, keepdims=True)
     values = select_rows(place_ref[...], to_slots(tiles))
-    values = weight_ref[...] * values + weight_partner_ref[...] * partner(values)
+    weight = weight_ref[...]
+    values = weight * values + (1.0 - weight) * partner(values)
     back = select_rows(slot_ref[...], values)
     for k in range(3):
-        tile = from_slots(back, k)
-        if k == 0:
-            tile = jnp.where(iota((64, 128), 1) == 6, inner, tile)
-        out_ref[:, 0, k * 128 : k * 128 + 128] = tile
-
-
-def unpack_kernel(in_ref, out_ref, inner_ref):
-    inner_ref[...] = in_ref[0:1, 0, 6:7]
+        out_ref[:, 0, k * 128 : k * 128 + 128] = from_slots(back, k)
+
+
+def unpack_kernel(in_ref, sum_ref, far_ref, out_ref, inner_ref):
+    inner_ref[...] = (sum_ref[...] + far_ref[...])[:, 6:7]
     faces = unpack_faces([in_ref[:, 0, k * 128 : k * 128 + 128] for k in range(3)])
     for f in range(6):
         out_ref[f] = jnp.concatenate([faces[s][f : f + 1, :] for s in range(4)], axis=0)
@@ -376,11 +369,11 @@
     return lax.all_to_all(values, axes, 0, 0)
 
 
+def from_ahead(values, ahead):
+    return lax.ppermute(values, "crs", [(y, (y - ahead) % 4) for y in range(4)])
+
+
 def body(residual, stiffness, solid, inverses, coarse_basis, assign, corners, coarse_inverse):
-    others = [
-        lax.ppermute(coarse_inverse, "crs", [(y, (y - ahead) % 4) for y in range(4)])
-        for ahead in (1, 2, 3)
-    ]
     basis_rows = coarse_basis.transpose(0, 2, 1, 3).reshape(576, 768)
     dma = pltpu.SemaphoreType.DMA
 
@@ -404,65 +397,72 @@
         residual.transpose(1, 0, 2),
         stiffness.transpose(1, 0, 2),
     )
-    weighed, weight, weight_partner, to_place, from_place, vertex = call(
+    own_columns, basis_here = call(
+        columns_kernel,
+        [VMEM, HBM, HBM, HBM],
+        [shaped(192, 384), VMEM((576, 768), BF16)],
+        "columns",
+        [VMEM((192, 768), F32), SMEM((4, 8), jnp.int32), dma((3,))],
+    )(solid_row, coarse_inverse, corners, basis_rows)
+    arrived, own_columns, basis_here = lax.optimization_barrier(
+        (exchange(packed, "sub"), own_columns, basis_here)
+    )
+    weighed, weight, to_place, from_place, vertex = call(
         weigh_kernel,
         [VMEM],
         [
             shaped(64, 1, 384),
             shaped(256, 128),
-            shaped(256, 128),
             shaped(256, 256, dtype=BF16),
             shaped(256, 256, dtype=BF16),
-            shaped(256, 128),
+            shaped(1, 256),
         ],
         "weigh",
-    )(exchange(packed, "sub"))
-    whole = [pl.BlockSpec(memory_space=VMEM), pl.BlockSpec(memory_space=HBM)]
+    )(arrived)
+    others = [from_ahead(own_columns, k) for k in (1, 2, 3)]
+    received = exchange(weighed, "sub")
+    message, rhs = call(
+        parts_kernel,
+        [VMEM] * 3,
+        [shaped(256, 1, 128), shaped(768, 128, dtype=BF16)],
+        "parts",
+    )(received, solid_row, basis_here)
+    whole = pl.BlockSpec(memory_space=VMEM)
     rows = 4608 // STEPS
-    local, message = pl.pallas_call(
+    local, inner_part = pl.pallas_call(
         solve_kernel,
         grid=(STEPS,),
-        in_specs=[whole[0], whole[0], pl.BlockSpec((rows, 768), lambda i: (i, 0)), whole[1]],
-        out_specs=(whole[0], whole[0]),
-        out_shape=(shaped(192, 128), shaped(256, 1, 128)),
-        scratch_shapes=[
-            VMEM((576, 768), BF16),
-            VMEM((768, 128), BF16),
-            VMEM((192, 128), F32),
-            dma(()),
-        ],
+        in_specs=[whole, whole, whole, pl.BlockSpec((rows, 768), lambda i: (i, 0))],
+        out_specs=(whole, whole),
+        out_shape=(shaped(192, 128), shaped(1, 128)),
         name="solve",
         compiler_params=pltpu.CompilerParams(vmem_limit_bytes=16 * 2**20),
     )(
-        exchange(weighed, "sub"),
+        received,
         solid_row,
+        rhs,
         pltpu.with_memory_space_constraint(inverses.reshape(4608, 768), HBM),
-        pltpu.with_memory_space_constraint(basis_rows, HBM),
     )
     (picked,) = call(
-        pick_kernel,
-        [VMEM] * 5 + [HBM] * 2,
-        [shaped(768, 128)],
-        "pick",
-        [
-            VMEM((192, 768), F32),
-            SMEM((4, 8), jnp.int32),
-            VMEM((768, 128), F32),
-            dma((2,)),
-        ],
-    )(local, vertex, *others, coarse_inverse, corners)
-    (solved,) = call(
-        coarse_kernel,
-        [VMEM] * 5 + [HBM],
-        [shaped(64, 1, 384)],
-        "coarse",
-        [VMEM((576, 768), BF16), dma(())],
-    )(exchange(message, ("crs", "sub")), to_place, picked, local, solid_row, basis_rows)
-    (averaged,) = call(average_kernel, [VMEM] * 5, [shaped(64, 1, 384)], "average")(
-        exchange(solved, "sub"), to_place, from_place, weight, weight_partner
-    )
-    out, inner = call(unpack_kernel, [VMEM], [shaped(6, 4, 768), shaped(1, 1)], "unpack")(
-        exchange(averaged, "sub")
+        pick_kernel, [VMEM] * 6, [shaped(768, 128)], "pick", [VMEM((768, 384), F32)]
+    )(rhs, vertex, own_columns, *others)
+    inner_near = lax.ppermute(inner_part, "crs", [(y, y ^ 1) for y in range(4)])
+    (solved,) = call(coarse_kernel, [VMEM] * 8, [shaped(64, 1, 384)], "coarse")(
+        exchange(message, ("crs", "sub")),
+        to_place,
+        picked,
+        local,
+        inner_part,
+        inner_near,
+        solid_row,
+        basis_here,
+    )
+    averaged, inner_sum = call(
+        average_kernel, [VMEM] * 4, [shaped(64, 1, 384), shaped(1, 128)], "average"
+    )(exchange(solved, "sub"), to_place, from_place, weight)
+    inner_far = lax.ppermute(inner_sum, "crs", [(y, y ^ 2) for y in range(4)])
+    out, inner = call(unpack_kernel, [VMEM] * 3, [shaped(6, 4, 768), shaped(1, 1)], "unpack")(
+        exchange(averaged, "sub"), inner_sum, inner_far
     )
     return out.transpose(1, 0, 2), inner.reshape(1)
 

time: 102 us -> 100 us (0.980)
  blocking collectives: 44.4 us -> 16.2 us
  starting transfers between devices: 24.5 us -> 39.6 us
  waiting for transfers between devices: 16.3 us -> 27.9 us
    all_to_all x3 -> x1, blocking collectives: 44.4 us -> 16.2 us  [exchange(): return lax.all_to_all(values, axes, 0, 0)]
    all_to_all x2 -> x4, waiting for transfers between devices: 16.3 us -> 26.9 us  [exchange(): return lax.all_to_all(values, axes, 0, 0)]
    all_to_all x2 -> x4, starting transfers between devices: 20 us -> 30.2 us  [exchange(): return lax.all_to_all(values, axes, 0, 0)]
    ppermute x3 -> x5, starting transfers between devices: 4.47 us -> 9.4 us  [the longest x3 5.06 us: from_ahead(): return lax.ppermute(values, 'crs', [(y, (y - ahead) % 4) for y in range(4)])]
    pallas_call x1, Pallas kernels: 5.47 us -> 4.34 us  [body(): pl.pallas_call(solve_kernel, grid=(STEPS,), in_specs=[whole, whole, whole...]
    pallas_call x6 -> x8, Pallas kernels: 10.2 us -> 11.3 us  [placed(): run(*(pltpu.with_memory_space_constraint(value, space) if space is HBM el...]
    ppermute x3 -> x5, waiting for transfers between devices: 0.01 us -> 1.08 us  [the longest x1 1.07 us: body(): inner_far = lax.ppermute(inner_sum, 'crs', [(y, y ^ 2) for y in range(4)])]
  transfers between devices with their start and end apart: 5 -> 9, of which waited for: 2 -> 5; matrix products, arithmetic and copies ran while one was open for 0% -> 0% of each run, Pallas kernels for 9% -> 8%
where the time goes in v4:
time: 100 us
  starting transfers between devices  39.6 us (40%)
  waiting for transfers between devices  27.9 us (28%)
  blocking collectives  16.2 us (16%)
  Pallas kernels  15.7 us (16%)
    all_to_all x4, starting transfers between devices, exchange(): return lax.all_to_all(values, axes, 0, 0)  30.2 us
    all_to_all x4, waiting for transfers between devices, exchange(): return lax.all_to_all(values, axes, 0, 0)  26.9 us
    all_to_all x1, blocking collectives, exchange(): return lax.all_to_all(values, axes, 0, 0)  16.2 us
    pallas_call x8, Pallas kernels, placed(): run(*(pltpu.with_memory_space_constraint(value, space) if space is HBM el...  11.3 us
    ppermute x3, starting transfers between devices, from_ahead(): return lax.ppermute(values, 'crs', [(y, (y - ahead) % 4) for y in range(4)])  5.06 us
    pallas_call x1, Pallas kernels, body(): pl.pallas_call(solve_kernel, grid=(STEPS,), in_specs=[whole, whole, whole...  4.34 us
    ppermute x1, starting transfers between devices, body(): inner_far = lax.ppermute(inner_sum, 'crs', [(y, y ^ 2) for y in range(4)])  2.91 us
  transfers between devices with their start and end apart: 9, of which 5 were waited for; matrix products, arithmetic and copies ran while one was open for 0% of the time, Pallas kernels for 8%

profile of v4, /device:TPU:1, one launch (start us, length us, event | category | flops | bytes accessed | tf_op | source)
XLA Modules:
  0.0 100.0 jit_solution(14981404614358418558)
XLA Ops:
  0.6 2.0 %pack.1 = (f32[64,1,768]{2,1,0:T(1,128)}, f32[1,128]{1,0:T(1,128)S(1)}) custom-call(s32[256]{0:T(256)} %assign_hbm.1, s32[4,8]{1,0:T(4,128)} %corners_hbm.3, s32[4,4,6]{2,1,0:T(4,128)} %bitcast.13, f32[6,4,768]{2,1,0:T(4,128)} %bitcast.11, f32[6,4,768]{2,1,0:T(4,128)} %bitcast.12), custom_call_target="tpu_custom_call" | custom-call | tf_op jit(solution)/shard_map/pack/pallas_call | solution.py:358
  2.6 13.0 %all-to-all-start = ((f32[64,1,768]{2,1,0:T(1,128)}), f32[64,1,768]{2,1,0:T(1,128)S(1)}, u32[]{:S(2)}, u32[]{:S(2)}) async-start(f32[64,1,768]{2,1,0:T(1,128)} %get-tuple-element.22), calls=%async_computation | async-start | bytes 393216 | tf_op jit(solution)/shard_map/all_to_all | solution.py:369
  15.6 1.5 %columns.1 = (f32[192,384]{1,0:T(8,128)S(1)}, bf16[576,768]{1,0:T(8,128)(2,1)S(1)}) custom-call(f32[1,128]{1,0:T(1,128)S(1)} %get-tuple-element.23.after_ref.solid_ref, f32[192,768]{1,0:T(8,128)} %inverse_hbm.1, s32[4,8]{1,0:T(4,128)} %corners_hbm.3, bf16[576,768]{1,0:T(8,128)(2,1)} %bitcast.10), custom_call_target="tpu_custom_call" | custom-call | tf_op jit(solution)/shard_map/columns/pallas_call | solution.py:358
  17.1 9.4 %all-to-all-done.in_ref = f32[64,1,768]{2,1,0:T(1,128)S(1)} async-done(((f32[64,1,768]{2,1,0:T(1,128)}), f32[64,1,768]{2,1,0:T(1,128)S(1)}, u32[]{:S(2)}, u32[]{:S(2)}) %all-to-all-start) | async-done | bytes 196640 | tf_op jit(solution)/shard_map/all_to_all | solution.py:369
  26.6 1.8 %weigh.1 = (f32[64,1,384]{2,1,0:T(1,128)}, f32[256,128]{1,0:T(8,128)S(1)}, bf16[256,256]{1,0:T(8,128)(2,1)S(1)}, bf16[256,256]{1,0:T(8,128)(2,1)S(1)}, f32[1,256]{1,0:T(1,128)S(1)}) custom-call(f32[64,1,768]{2,1,0:T(1,128)S(1)} %all-to-all-done.in_ref), custom_call_target="tpu_custom_call" | custom-call | tf_op jit(solution)/shard_map/weigh/pallas_call | solution.py:358
  28.4 5.7 %all-to-all-start.1 = ((f32[64,1,384]{2,1,0:T(1,128)}), f32[64,1,384]{2,1,0:T(1,128)S(1)}, u32[]{:S(2)}, u32[]{:S(2)}) async-start(f32[64,1,384]{2,1,0:T(1,128)} %get-tuple-element.27), calls=%async_computation.1 | async-start | bytes 196608 | tf_op jit(solution)/shard_map/all_to_all | solution.py:369
  34.1 1.4 %collective-permute-start.2 = (f32[192,384]{1,0:T(8,128)S(1)}, f32[192,384]{1,0:T(8,128)S(1)}, u32[]{:S(2)}, u32[]{:S(2)}) collective-permute-start(f32[192,384]{1,0:T(8,128)S(1)} %get-tuple-element.33.own_ref), channel_id=1, source_target_pairs={{0,1},{1,2},{2,3},{3,0},{4,5},{5,6},{6,7},{7,4},{8,9},{9,10},{10,1... | collective-permute-start | bytes 884744 | tf_op jit(solution)/shard_map/ppermute | solution.py:373
  35.5 2.6 %collective-permute-start.1 = (f32[192,384]{1,0:T(8,128)S(1)}, f32[192,384]{1,0:T(8,128)S(1)}, u32[]{:S(2)}, u32[]{:S(2)}) collective-permute-start(f32[192,384]{1,0:T(8,128)S(1)} %get-tuple-element.33.own_ref), channel_id=1, source_target_pairs={{0,2},{1,3},{2,0},{3,1},{4,6},{5,7},{6,4},{7,5},{8,10},{9,11},{10,... | collective-permute-start | bytes 884744 | tf_op jit(solution)/shard_map/ppermute | solution.py:373
  38.1 1.1 %collective-permute-start = (f32[192,384]{1,0:T(8,128)S(1)}, f32[192,384]{1,0:T(8,128)S(1)}, u32[]{:S(2)}, u32[]{:S(2)}) collective-permute-start(f32[192,384]{1,0:T(8,128)S(1)} %get-tuple-element.33.own_ref), channel_id=1, source_target_pairs={{0,3},{1,0},{2,1},{3,2},{4,7},{5,4},{6,5},{7,6},{8,11},{9,8},{10,9... | collective-permute-start | bytes 884744 | tf_op jit(solution)/shard_map/ppermute | solution.py:373
  39.2 5.1 %all-to-all-done.1.in_ref = f32[64,1,384]{2,1,0:T(1,128)S(1)} async-done(((f32[64,1,384]{2,1,0:T(1,128)}), f32[64,1,384]{2,1,0:T(1,128)S(1)}, u32[]{:S(2)}, u32[]{:S(2)}) %all-to-all-start.1) | async-done | bytes 98336 | tf_op jit(solution)/shard_map/all_to_all | solution.py:369
  44.3 1.3 %parts.1 = (f32[256,1,128]{2,1,0:T(1,128)}, bf16[768,128]{1,0:T(8,128)(2,1)S(1)}) custom-call(f32[64,1,384]{2,1,0:T(1,128)S(1)} %all-to-all-done.1.in_ref, f32[1,128]{1,0:T(1,128)S(1)} %get-tuple-element.23.after_ref.solid_ref, bf16[576,768]{1,0:T(8,128)(2,1)S(1)} %get-tuple-element.28.basis.basis_ref), custom_call_target="tpu_custom_call" | custom-call | tf_op jit(solution)/shard_map/parts/pallas_call | solution.py:358
  45.6 7.0 %all-to-all-start.2 = ((f32[256,1,128]{2,1,0:T(1,128)}), f32[256,1,128]{2,1,0:T(1,128)S(1)}, u32[]{:S(2)}, u32[]{:S(2)}) async-start(f32[256,1,128]{2,1,0:T(1,128)} %get-tuple-element.29), calls=%async_computation.2 | async-start | bytes 262144 | tf_op jit(solution)/shard_map/all_to_all | solution.py:369
  52.6 4.3 %solve.1 = (f32[192,128]{1,0:T(8,128)S(1)}, f32[1,128]{1,0:T(1,128)S(1)}) custom-call(f32[64,1,384]{2,1,0:T(1,128)S(1)} %all-to-all-done.1.in_ref, f32[1,128]{1,0:T(1,128)S(1)} %get-tuple-element.23.after_ref.solid_ref, bf16[768,128]{1,0:T(8,128)(2,1)S(1)} %get-tuple-element.31.after_ref.rhs, bf16[4608,768]{1,0:T(8,128)(2,1)} %bitcast.9), custom_call_target="tpu_custom_call" | custom-call | tf_op jit(solution)/shard_map/solve/pallas_call | solution.py:432
  56.9 1.4 %collective-permute-start.3 = (f32[1,128]{1,0:T(1,128)S(1)}, f32[1,128]{1,0:T(1,128)S(1)}, u32[]{:S(2)}, u32[]{:S(2)}) collective-permute-start(f32[1,128]{1,0:T(1,128)S(1)} %get-tuple-element.35.inner_ref), channel_id=1, source_target_pairs={{0,1},{1,0},{2,3},{3,2},{4,5},{5,4},{6,7},{7,6},{8,9},{9,8},{10,11... | collective-permute-start | bytes 1544 | tf_op jit(solution)/shard_map/ppermute | solution.py:449
  58.4 0.0 collective-permute-done.2.three_ref
  58.4 0.0 collective-permute-done.1.two_ref
  58.4 0.0 collective-permute-done.one_ref
  58.4 1.1 %pick.1.picked_ref = f32[768,128]{1,0:T(8,128)S(1)} custom-call(bf16[768,128]{1,0:T(8,128)(2,1)S(1)} %get-tuple-element.31.after_ref.rhs, f32[1,256]{1,0:T(1,128)S(1)} %get-tuple-element.32.vertex_ref, f32[192,384]{1,0:T(8,128)S(1)} %get-tuple-element.33.own_ref, f32[192,384]{1,0:T(8,128)S(1)} %collective-permute-done.one_ref, ...), custom_call_target="tpu_custom_call" | custom-call | tf_op jit(solution)/shard_map/pick/pallas_call | solution.py:358
  59.5 0.0 collective-permute-done.3.near_ref
  59.5 6.0 %all-to-all-done.2.in_ref = f32[256,1,128]{2,1,0:T(1,128)S(1)} async-done(((f32[256,1,128]{2,1,0:T(1,128)}), f32[256,1,128]{2,1,0:T(1,128)S(1)}, u32[]{:S(2)}, u32[]{:S(2)}) %all-to-all-start.2) | async-done | bytes 131104 | tf_op jit(solution)/shard_map/all_to_all | solution.py:369
  65.5 1.4 %coarse.1 = f32[64,1,384]{2,1,0:T(1,128)S(1)} custom-call(f32[256,1,128]{2,1,0:T(1,128)S(1)} %all-to-all-done.2.in_ref, bf16[256,256]{1,0:T(8,128)(2,1)S(1)} %get-tuple-element.30.place_ref, f32[768,128]{1,0:T(8,128)S(1)} %pick.1.picked_ref, f32[192,128]{1,0:T(8,128)S(1)} %get-tuple-element.34.local_ref, f32[1,128]{1,0:T(1,128)S(1)} %get-tuple-element.35.inner_ref, ...), custom_call_target="tpu_custom_call" | custom-call | tf_op jit(solution)/shard_map/coarse/pallas_call | solution.py:358
  66.8 16.2 %all_to_all.25.in_ref = f32[64,1,384]{2,1,0:T(1,128)S(1)} all-to-all(f32[64,1,384]{2,1,0:T(1,128)S(1)} %coarse.1), channel_id=1, replica_groups=mesh['sub'=64,'crs'=4] {'sub'}, dimensions={0} | all-to-all | bytes 196608 | tf_op jit(solution)/shard_map/all_to_all | solution.py:369
  83.0 1.4 %average.1 = (f32[64,1,384]{2,1,0:T(1,128)}, f32[1,128]{1,0:T(1,128)S(1)}) custom-call(f32[64,1,384]{2,1,0:T(1,128)S(1)} %all_to_all.25.in_ref, bf16[256,256]{1,0:T(8,128)(2,1)S(1)} %get-tuple-element.30.place_ref, bf16[256,256]{1,0:T(8,128)(2,1)S(1)} %get-tuple-element.36.slot_ref, f32[256,128]{1,0:T(8,128)S(1)} %get-tuple-element.37.weight_ref), custom_call_target="tpu_custom_call" | custom-call | tf_op jit(solution)/shard_map/average/pallas_call | solution.py:358
  84.5 4.4 %all-to-all-start.4 = ((f32[64,1,384]{2,1,0:T(1,128)}), f32[64,1,384]{2,1,0:T(1,128)S(1)}, u32[]{:S(2)}, u32[]{:S(2)}) async-start(f32[64,1,384]{2,1,0:T(1,128)} %get-tuple-element.38), calls=%async_computation.4 | async-start | bytes 196608 | tf_op jit(solution)/shard_map/all_to_all | solution.py:369
  88.9 2.9 %collective-permute-start.4 = (f32[1,128]{1,0:T(1,128)S(1)}, f32[1,128]{1,0:T(1,128)S(1)}, u32[]{:S(2)}, u32[]{:S(2)}) collective-permute-start(f32[1,128]{1,0:T(1,128)S(1)} %get-tuple-element.39.sum_ref), channel_id=1, source_target_pairs={{0,2},{1,3},{2,0},{3,1},{4,6},{5,7},{6,4},{7,5},{8,10},{9,11},{10,... | collective-permute-start | bytes 1544 | tf_op jit(solution)/shard_map/ppermute | solution.py:463
  91.8 1.1 %collective-permute-done.4.far_ref = f32[1,128]{1,0:T(1,128)S(1)} collective-permute-done((f32[1,128]{1,0:T(1,128)S(1)}, f32[1,128]{1,0:T(1,128)S(1)}, u32[]{:S(2)}, u32[]{:S(2)}) %collective-permute-start.4) | collective-permute-done | bytes 544 | tf_op jit(solution)/shard_map/ppermute | solution.py:463
  92.9 6.3 %all-to-all-done.4.in_ref = f32[64,1,384]{2,1,0:T(1,128)S(1)} async-done(((f32[64,1,384]{2,1,0:T(1,128)}), f32[64,1,384]{2,1,0:T(1,128)S(1)}, u32[]{:S(2)}, u32[]{:S(2)}) %all-to-all-start.4) | async-done | bytes 98336 | tf_op jit(solution)/shard_map/all_to_all | solution.py:369
  99.2 0.8 unpack.1
Async XLA Ops:
  2.6 23.9 %all-to-all-start = ((f32[64,1,768]{2,1,0:T(1,128)}), f32[64,1,768]{2,1,0:T(1,128)S(1)}, u32[]{:S(2)}, u32[]{:S(2)}) async-start(f32[64,1,768]{2,1,0:T(1,128)} %get-tuple-element.22), calls=%async_computation | async-start | bytes 393216 | tf_op jit(solution)/shard_map/all_to_all | solution.py:369
  28.4 15.9 %all-to-all-start.1 = ((f32[64,1,384]{2,1,0:T(1,128)}), f32[64,1,384]{2,1,0:T(1,128)S(1)}, u32[]{:S(2)}, u32[]{:S(2)}) async-start(f32[64,1,384]{2,1,0:T(1,128)} %get-tuple-element.27), calls=%async_computation.1 | async-start | bytes 196608 | tf_op jit(solution)/shard_map/all_to_all | solution.py:369
  34.1 24.3 %collective-permute-start.2 = (f32[192,384]{1,0:T(8,128)S(1)}, f32[192,384]{1,0:T(8,128)S(1)}, u32[]{:S(2)}, u32[]{:S(2)}) collective-permute-start(f32[192,384]{1,0:T(8,128)S(1)} %get-tuple-element.33.own_ref), channel_id=1, source_target_pairs={{0,1},{1,2},{2,3},{3,0},{4,5},{5,6},{6,7},{7,4},{8,9},{9,10},{10,1... | collective-permute-start | bytes 884744 | tf_op jit(solution)/shard_map/ppermute | solution.py:373
  35.5 22.9 %collective-permute-start.1 = (f32[192,384]{1,0:T(8,128)S(1)}, f32[192,384]{1,0:T(8,128)S(1)}, u32[]{:S(2)}, u32[]{:S(2)}) collective-permute-start(f32[192,384]{1,0:T(8,128)S(1)} %get-tuple-element.33.own_ref), channel_id=1, source_target_pairs={{0,2},{1,3},{2,0},{3,1},{4,6},{5,7},{6,4},{7,5},{8,10},{9,11},{10,... | collective-permute-start | bytes 884744 | tf_op jit(solution)/shard_map/ppermute | solution.py:373
  38.1 20.3 %collective-permute-start = (f32[192,384]{1,0:T(8,128)S(1)}, f32[192,384]{1,0:T(8,128)S(1)}, u32[]{:S(2)}, u32[]{:S(2)}) collective-permute-start(f32[192,384]{1,0:T(8,128)S(1)} %get-tuple-element.33.own_ref), channel_id=1, source_target_pairs={{0,3},{1,0},{2,1},{3,2},{4,7},{5,4},{6,5},{7,6},{8,11},{9,8},{10,9... | collective-permute-start | bytes 884744 | tf_op jit(solution)/shard_map/ppermute | solution.py:373
  45.6 19.9 %all-to-all-start.2 = ((f32[256,1,128]{2,1,0:T(1,128)}), f32[256,1,128]{2,1,0:T(1,128)S(1)}, u32[]{:S(2)}, u32[]{:S(2)}) async-start(f32[256,1,128]{2,1,0:T(1,128)} %get-tuple-element.29), calls=%async_computation.2 | async-start | bytes 262144 | tf_op jit(solution)/shard_map/all_to_all | solution.py:369
  56.9 2.5 %collective-permute-start.3 = (f32[1,128]{1,0:T(1,128)S(1)}, f32[1,128]{1,0:T(1,128)S(1)}, u32[]{:S(2)}, u32[]{:S(2)}) collective-permute-start(f32[1,128]{1,0:T(1,128)S(1)} %get-tuple-element.35.inner_ref), channel_id=1, source_target_pairs={{0,1},{1,0},{2,3},{3,2},{4,5},{5,4},{6,7},{7,6},{8,9},{9,8},{10,11... | collective-permute-start | bytes 1544 | tf_op jit(solution)/shard_map/ppermute | solution.py:449
  84.5 14.7 %all-to-all-start.4 = ((f32[64,1,384]{2,1,0:T(1,128)}), f32[64,1,384]{2,1,0:T(1,128)S(1)}, u32[]{:S(2)}, u32[]{:S(2)}) async-start(f32[64,1,384]{2,1,0:T(1,128)} %get-tuple-element.38), calls=%async_computation.4 | async-start | bytes 196608 | tf_op jit(solution)/shard_map/all_to_all | solution.py:369
  88.9 4.0 %collective-permute-start.4 = (f32[1,128]{1,0:T(1,128)S(1)}, f32[1,128]{1,0:T(1,128)S(1)}, u32[]{:S(2)}, u32[]{:S(2)}) collective-permute-start(f32[1,128]{1,0:T(1,128)S(1)} %get-tuple-element.39.sum_ref), channel_id=1, source_target_pairs={{0,2},{1,3},{2,0},{3,1},{4,6},{5,7},{6,4},{7,5},{8,10},{9,11},{10,... | collective-permute-start | bytes 1544 | tf_op jit(solution)/shard_map/ppermute | solution.py:463

commit v5 on v4

--- a/solution.py
+++ b/solution.py
@@ -276,7 +276,7 @@
 
 
 def coarse_kernel(
-    in_ref, place_ref, picked_ref, local_ref, inner_ref, near_ref, solid_ref, basis_ref, out_ref
+    in_ref, place_ref, picked_ref, local_ref, inner_ref, solid_ref, basis_ref, out_ref
 ):
     summed = in_ref[0:64, 0, :]
     me = lax.axis_index("sub")
@@ -297,7 +297,7 @@
         terms = terms + picked_ref[j * 256 : j * 256 + 256, :] * parts[:, j : j + 1]
     rounded = jnp.sum(terms, axis=0, keepdims=True).astype(BF16).astype(F32)
     inner = jnp.sum(rounded * mine, axis=1, keepdims=True)
-    inner = (inner_ref[...] + near_ref[...]) + 0.5 * inner
+    inner = inner_ref[...] + 0.25 * inner
     values = jnp.broadcast_to(rounded, (128, 128)).T
     faces = []
     for s in range(4):
@@ -328,8 +328,9 @@
         out_ref[:, 0, k * 128 : k * 128 + 128] = from_slots(back, k)
 
 
-def unpack_kernel(in_ref, sum_ref, far_ref, out_ref, inner_ref):
-    inner_ref[...] = (sum_ref[...] + far_ref[...])[:, 6:7]
+def unpack_kernel(in_ref, sum_ref, one_ref, two_ref, three_ref, out_ref, inner_ref):
+    inner = (sum_ref[...] + two_ref[...]) + (one_ref[...] + three_ref[...])
+    inner_ref[...] = inner[:, 6:7]
     faces = unpack_faces([in_ref[:, 0, k * 128 : k * 128 + 128] for k in range(3)])
     for f in range(6):
         out_ref[f] = jnp.concatenate([faces[s][f : f + 1, :] for s in range(4)], axis=0)
@@ -446,23 +447,20 @@
     (picked,) = call(
         pick_kernel, [VMEM] * 6, [shaped(768, 128)], "pick", [VMEM((768, 384), F32)]
     )(rhs, vertex, own_columns, *others)
-    inner_near = lax.ppermute(inner_part, "crs", [(y, y ^ 1) for y in range(4)])
-    (solved,) = call(coarse_kernel, [VMEM] * 8, [shaped(64, 1, 384)], "coarse")(
+    (solved,) = call(coarse_kernel, [VMEM] * 7, [shaped(64, 1, 384)], "coarse")(
         exchange(message, ("crs", "sub")),
         to_place,
         picked,
         local,
         inner_part,
-        inner_near,
         solid_row,
         basis_here,
     )
     averaged, inner_sum = call(
         average_kernel, [VMEM] * 4, [shaped(64, 1, 384), shaped(1, 128)], "average"
     )(exchange(solved, "sub"), to_place, from_place, weight)
-    inner_far = lax.ppermute(inner_sum, "crs", [(y, y ^ 2) for y in range(4)])
-    out, inner = call(unpack_kernel, [VMEM] * 3, [shaped(6, 4, 768), shaped(1, 1)], "unpack")(
-        exchange(averaged, "sub"), inner_sum, inner_far
+    out, inner = call(unpack_kernel, [VMEM] * 5, [shaped(6, 4, 768), shaped(1, 1)], "unpack")(
+        exchange(averaged, "sub"), inner_sum, *(from_ahead(inner_sum, k) for k in (1, 2, 3))
     )
     return out.transpose(1, 0, 2), inner.reshape(1)
 

time: 100 us -> 98.6 us (0.986)
  blocking collectives: 16.2 us -> 14.4 us
    ppermute x2 -> x0, starting transfers between devices: 4.33 us -> none  [the longest x1 2.91 us: body(): inner_far = lax.ppermute(inner_sum, 'crs', [(y, y ^ 2) for y in range(4)])]
    ppermute x3 -> x6, starting transfers between devices: 5.06 us -> 9.33 us  [from_ahead(): return lax.ppermute(values, 'crs', [(y, (y - ahead) % 4) for y in range(4)])]
    all_to_all x1, blocking collectives: 16.2 us -> 14.4 us  [exchange(): return lax.all_to_all(values, axes, 0, 0)]
    ppermute x3 -> x6, waiting for transfers between devices: 0.01 us -> 1.58 us  [from_ahead(): return lax.ppermute(values, 'crs', [(y, (y - ahead) % 4) for y in range(4)])]
    ppermute x2 -> x0, waiting for transfers between devices: 1.08 us -> none  [the longest x1 1.07 us: body(): inner_far = lax.ppermute(inner_sum, 'crs', [(y, y ^ 2) for y in range(4)])]
  transfers between devices with their start and end apart: 9 -> 10, of which waited for: 5 -> 6; matrix products, arithmetic and copies ran while one was open for 0% -> 0% of each run, Pallas kernels for 8% -> 8%
where the time goes in v5:
time: 98.6 us; the launch traced here: 98.2 us
  starting transfers between devices  39.6 us (40%)
  waiting for transfers between devices  27.9 us (28%)
  Pallas kernels  15.7 us (16%)
  blocking collectives  14.4 us (15%)
    all_to_all x4, starting transfers between devices, exchange(): return lax.all_to_all(values, axes, 0, 0)  30.2 us
    all_to_all x4, waiting for transfers between devices, exchange(): return lax.all_to_all(values, axes, 0, 0)  26.3 us
    all_to_all x1, blocking collectives, exchange(): return lax.all_to_all(values, axes, 0, 0)  14.4 us
    pallas_call x8, Pallas kernels, placed(): run(*(pltpu.with_memory_space_constraint(value, space) if space is HBM el...  11.3 us
    ppermute x6, starting transfers between devices, from_ahead(): return lax.ppermute(values, 'crs', [(y, (y - ahead) % 4) for y in range(4)])  9.33 us
    pallas_call x1, Pallas kernels, body(): pl.pallas_call(solve_kernel, grid=(STEPS,), in_specs=[whole, whole, whole...  4.34 us
  transfers between devices with their start and end apart: 10, of which 6 were waited for; matrix products, arithmetic and copies ran while one was open for 0% of the time, Pallas kernels for 8%

profile of v5, /device:TPU:1, one launch (start us, length us, event | category | flops | bytes accessed | tf_op | source)
XLA Modules:
  0.0 98.2 jit_solution(420876006916006859)
XLA Ops:
  0.6 2.0 %pack.1 = (f32[64,1,768]{2,1,0:T(1,128)}, f32[1,128]{1,0:T(1,128)S(1)}) custom-call(s32[256]{0:T(256)} %assign_hbm.1, s32[4,8]{1,0:T(4,128)} %corners_hbm.3, s32[4,4,6]{2,1,0:T(4,128)} %bitcast.13, f32[6,4,768]{2,1,0:T(4,128)} %bitcast.11, f32[6,4,768]{2,1,0:T(4,128)} %bitcast.12), custom_call_target="tpu_custom_call" | custom-call | tf_op jit(solution)/shard_map/pack/pallas_call | solution.py:359
  2.6 13.0 %all-to-all-start = ((f32[64,1,768]{2,1,0:T(1,128)}), f32[64,1,768]{2,1,0:T(1,128)S(1)}, u32[]{:S(2)}, u32[]{:S(2)}) async-start(f32[64,1,768]{2,1,0:T(1,128)} %get-tuple-element.22), calls=%async_computation | async-start | bytes 393216 | tf_op jit(solution)/shard_map/all_to_all | solution.py:370
  15.6 1.5 %columns.1 = (f32[192,384]{1,0:T(8,128)S(1)}, bf16[576,768]{1,0:T(8,128)(2,1)S(1)}) custom-call(f32[1,128]{1,0:T(1,128)S(1)} %get-tuple-element.23.after_ref.solid_ref, f32[192,768]{1,0:T(8,128)} %inverse_hbm.1, s32[4,8]{1,0:T(4,128)} %corners_hbm.3, bf16[576,768]{1,0:T(8,128)(2,1)} %bitcast.10), custom_call_target="tpu_custom_call" | custom-call | tf_op jit(solution)/shard_map/columns/pallas_call | solution.py:359
  17.1 9.4 %all-to-all-done.in_ref = f32[64,1,768]{2,1,0:T(1,128)S(1)} async-done(((f32[64,1,768]{2,1,0:T(1,128)}), f32[64,1,768]{2,1,0:T(1,128)S(1)}, u32[]{:S(2)}, u32[]{:S(2)}) %all-to-all-start) | async-done | bytes 196640 | tf_op jit(solution)/shard_map/all_to_all | solution.py:370
  26.6 1.8 %weigh.1 = (f32[64,1,384]{2,1,0:T(1,128)}, f32[256,128]{1,0:T(8,128)S(1)}, bf16[256,256]{1,0:T(8,128)(2,1)S(1)}, bf16[256,256]{1,0:T(8,128)(2,1)S(1)}, f32[1,256]{1,0:T(1,128)S(1)}) custom-call(f32[64,1,768]{2,1,0:T(1,128)S(1)} %all-to-all-done.in_ref), custom_call_target="tpu_custom_call" | custom-call | tf_op jit(solution)/shard_map/weigh/pallas_call | solution.py:359
  28.4 5.7 %all-to-all-start.1 = ((f32[64,1,384]{2,1,0:T(1,128)}), f32[64,1,384]{2,1,0:T(1,128)S(1)}, u32[]{:S(2)}, u32[]{:S(2)}) async-start(f32[64,1,384]{2,1,0:T(1,128)} %get-tuple-element.27), calls=%async_computation.1 | async-start | bytes 196608 | tf_op jit(solution)/shard_map/all_to_all | solution.py:370
  34.1 1.4 %collective-permute-start.2 = (f32[192,384]{1,0:T(8,128)S(1)}, f32[192,384]{1,0:T(8,128)S(1)}, u32[]{:S(2)}, u32[]{:S(2)}) collective-permute-start(f32[192,384]{1,0:T(8,128)S(1)} %get-tuple-element.33.own_ref), channel_id=1, source_target_pairs={{0,1},{1,2},{2,3},{3,0},{4,5},{5,6},{6,7},{7,4},{8,9},{9,10},{10,1... | collective-permute-start | bytes 884744 | tf_op jit(solution)/shard_map/ppermute | solution.py:374
  35.5 2.6 %collective-permute-start.1 = (f32[192,384]{1,0:T(8,128)S(1)}, f32[192,384]{1,0:T(8,128)S(1)}, u32[]{:S(2)}, u32[]{:S(2)}) collective-permute-start(f32[192,384]{1,0:T(8,128)S(1)} %get-tuple-element.33.own_ref), channel_id=1, source_target_pairs={{0,2},{1,3},{2,0},{3,1},{4,6},{5,7},{6,4},{7,5},{8,10},{9,11},{10,... | collective-permute-start | bytes 884744 | tf_op jit(solution)/shard_map/ppermute | solution.py:374
  38.1 1.1 %collective-permute-start = (f32[192,384]{1,0:T(8,128)S(1)}, f32[192,384]{1,0:T(8,128)S(1)}, u32[]{:S(2)}, u32[]{:S(2)}) collective-permute-start(f32[192,384]{1,0:T(8,128)S(1)} %get-tuple-element.33.own_ref), channel_id=1, source_target_pairs={{0,3},{1,0},{2,1},{3,2},{4,7},{5,4},{6,5},{7,6},{8,11},{9,8},{10,9... | collective-permute-start | bytes 884744 | tf_op jit(solution)/shard_map/ppermute | solution.py:374
  39.2 5.1 %all-to-all-done.1.in_ref = f32[64,1,384]{2,1,0:T(1,128)S(1)} async-done(((f32[64,1,384]{2,1,0:T(1,128)}), f32[64,1,384]{2,1,0:T(1,128)S(1)}, u32[]{:S(2)}, u32[]{:S(2)}) %all-to-all-start.1) | async-done | bytes 98336 | tf_op jit(solution)/shard_map/all_to_all | solution.py:370
  44.2 1.3 %parts.1 = (f32[256,1,128]{2,1,0:T(1,128)}, bf16[768,128]{1,0:T(8,128)(2,1)S(1)}) custom-call(f32[64,1,384]{2,1,0:T(1,128)S(1)} %all-to-all-done.1.in_ref, f32[1,128]{1,0:T(1,128)S(1)} %get-tuple-element.23.after_ref.solid_ref, bf16[576,768]{1,0:T(8,128)(2,1)S(1)} %get-tuple-element.28.basis.basis_ref), custom_call_target="tpu_custom_call" | custom-call | tf_op jit(solution)/shard_map/parts/pallas_call | solution.py:359
  45.5 7.1 %all-to-all-start.2 = ((f32[256,1,128]{2,1,0:T(1,128)}), f32[256,1,128]{2,1,0:T(1,128)S(1)}, u32[]{:S(2)}, u32[]{:S(2)}) async-start(f32[256,1,128]{2,1,0:T(1,128)} %get-tuple-element.29), calls=%async_computation.2 | async-start | bytes 262144 | tf_op jit(solution)/shard_map/all_to_all | solution.py:370
  52.6 4.3 %solve.1 = (f32[192,128]{1,0:T(8,128)S(1)}, f32[1,128]{1,0:T(1,128)S(1)}) custom-call(f32[64,1,384]{2,1,0:T(1,128)S(1)} %all-to-all-done.1.in_ref, f32[1,128]{1,0:T(1,128)S(1)} %get-tuple-element.23.after_ref.solid_ref, bf16[768,128]{1,0:T(8,128)(2,1)S(1)} %get-tuple-element.31.after_ref.rhs, bf16[4608,768]{1,0:T(8,128)(2,1)} %bitcast.9), custom_call_target="tpu_custom_call" | custom-call | tf_op jit(solution)/shard_map/solve/pallas_call | solution.py:433
  56.9 0.0 collective-permute-done.2.three_ref
  56.9 0.0 collective-permute-done.1.two_ref
  56.9 0.0 collective-permute-done.one_ref
  56.9 1.1 %pick.1.picked_ref = f32[768,128]{1,0:T(8,128)S(1)} custom-call(bf16[768,128]{1,0:T(8,128)(2,1)S(1)} %get-tuple-element.31.after_ref.rhs, f32[1,256]{1,0:T(1,128)S(1)} %get-tuple-element.32.vertex_ref, f32[192,384]{1,0:T(8,128)S(1)} %get-tuple-element.33.own_ref, f32[192,384]{1,0:T(8,128)S(1)} %collective-permute-done.one_ref, ...), custom_call_target="tpu_custom_call" | custom-call | tf_op jit(solution)/shard_map/pick/pallas_call | solution.py:359
  58.0 7.4 %all-to-all-done.2.in_ref = f32[256,1,128]{2,1,0:T(1,128)S(1)} async-done(((f32[256,1,128]{2,1,0:T(1,128)}), f32[256,1,128]{2,1,0:T(1,128)S(1)}, u32[]{:S(2)}, u32[]{:S(2)}) %all-to-all-start.2) | async-done | bytes 131104 | tf_op jit(solution)/shard_map/all_to_all | solution.py:370
  65.5 1.4 %coarse.1 = f32[64,1,384]{2,1,0:T(1,128)S(1)} custom-call(f32[256,1,128]{2,1,0:T(1,128)S(1)} %all-to-all-done.2.in_ref, bf16[256,256]{1,0:T(8,128)(2,1)S(1)} %get-tuple-element.30.place_ref, f32[768,128]{1,0:T(8,128)S(1)} %pick.1.picked_ref, f32[192,128]{1,0:T(8,128)S(1)} %get-tuple-element.34.local_ref, f32[1,128]{1,0:T(1,128)S(1)} %get-tuple-element.35.inner_ref, ...), custom_call_target="tpu_custom_call" | custom-call | tf_op jit(solution)/shard_map/coarse/pallas_call | solution.py:359
  66.8 14.4 %all_to_all.25.in_ref = f32[64,1,384]{2,1,0:T(1,128)S(1)} all-to-all(f32[64,1,384]{2,1,0:T(1,128)S(1)} %coarse.1), channel_id=1, replica_groups=mesh['sub'=64,'crs'=4] {'sub'}, dimensions={0} | all-to-all | bytes 196608 | tf_op jit(solution)/shard_map/all_to_all | solution.py:370
  81.3 1.5 %average.1 = (f32[64,1,384]{2,1,0:T(1,128)}, f32[1,128]{1,0:T(1,128)S(1)}) custom-call(f32[64,1,384]{2,1,0:T(1,128)S(1)} %all_to_all.25.in_ref, bf16[256,256]{1,0:T(8,128)(2,1)S(1)} %get-tuple-element.30.place_ref, bf16[256,256]{1,0:T(8,128)(2,1)S(1)} %get-tuple-element.36.slot_ref, f32[256,128]{1,0:T(8,128)S(1)} %get-tuple-element.37.weight_ref), custom_call_target="tpu_custom_call" | custom-call | tf_op jit(solution)/shard_map/average/pallas_call | solution.py:359
  82.7 4.4 %all-to-all-start.4 = ((f32[64,1,384]{2,1,0:T(1,128)}), f32[64,1,384]{2,1,0:T(1,128)S(1)}, u32[]{:S(2)}, u32[]{:S(2)}) async-start(f32[64,1,384]{2,1,0:T(1,128)} %get-tuple-element.38), calls=%async_computation.4 | async-start | bytes 196608 | tf_op jit(solution)/shard_map/all_to_all | solution.py:370
  87.2 0.6 collective-permute-start.5
  87.8 2.5 %collective-permute-start.4 = (f32[1,128]{1,0:T(1,128)S(1)}, f32[1,128]{1,0:T(1,128)S(1)}, u32[]{:S(2)}, u32[]{:S(2)}) collective-permute-start(f32[1,128]{1,0:T(1,128)S(1)} %get-tuple-element.39.sum_ref), channel_id=1, source_target_pairs={{0,2},{1,3},{2,0},{3,1},{4,6},{5,7},{6,4},{7,5},{8,10},{9,11},{10,... | collective-permute-start | bytes 1544 | tf_op jit(solution)/shard_map/ppermute | solution.py:374
  90.3 1.1 %collective-permute-start.3 = (f32[1,128]{1,0:T(1,128)S(1)}, f32[1,128]{1,0:T(1,128)S(1)}, u32[]{:S(2)}, u32[]{:S(2)}) collective-permute-start(f32[1,128]{1,0:T(1,128)S(1)} %get-tuple-element.39.sum_ref), channel_id=1, source_target_pairs={{0,3},{1,0},{2,1},{3,2},{4,7},{5,4},{6,5},{7,6},{8,11},{9,8},{10,9... | collective-permute-start | bytes 1544 | tf_op jit(solution)/shard_map/ppermute | solution.py:374
  91.4 0.0 collective-permute-done.5.three_ref
  91.4 0.5 collective-permute-done.4.two_ref
  92.0 1.0 %collective-permute-done.3.one_ref = f32[1,128]{1,0:T(1,128)S(1)} collective-permute-done((f32[1,128]{1,0:T(1,128)S(1)}, f32[1,128]{1,0:T(1,128)S(1)}, u32[]{:S(2)}, u32[]{:S(2)}) %collective-permute-start.3) | collective-permute-done | bytes 544 | tf_op jit(solution)/shard_map/ppermute | solution.py:374
  93.0 4.4 %all-to-all-done.4.in_ref = f32[64,1,384]{2,1,0:T(1,128)S(1)} async-done(((f32[64,1,384]{2,1,0:T(1,128)}), f32[64,1,384]{2,1,0:T(1,128)S(1)}, u32[]{:S(2)}, u32[]{:S(2)}) %all-to-all-start.4) | async-done | bytes 98336 | tf_op jit(solution)/shard_map/all_to_all | solution.py:370
  97.4 0.8 unpack.1
Async XLA Ops:
  2.6 23.9 %all-to-all-start = ((f32[64,1,768]{2,1,0:T(1,128)}), f32[64,1,768]{2,1,0:T(1,128)S(1)}, u32[]{:S(2)}, u32[]{:S(2)}) async-start(f32[64,1,768]{2,1,0:T(1,128)} %get-tuple-element.22), calls=%async_computation | async-start | bytes 393216 | tf_op jit(solution)/shard_map/all_to_all | solution.py:370
  28.4 15.8 %all-to-all-start.1 = ((f32[64,1,384]{2,1,0:T(1,128)}), f32[64,1,384]{2,1,0:T(1,128)S(1)}, u32[]{:S(2)}, u32[]{:S(2)}) async-start(f32[64,1,384]{2,1,0:T(1,128)} %get-tuple-element.27), calls=%async_computation.1 | async-start | bytes 196608 | tf_op jit(solution)/shard_map/all_to_all | solution.py:370
  34.1 22.8 %collective-permute-start.2 = (f32[192,384]{1,0:T(8,128)S(1)}, f32[192,384]{1,0:T(8,128)S(1)}, u32[]{:S(2)}, u32[]{:S(2)}) collective-permute-start(f32[192,384]{1,0:T(8,128)S(1)} %get-tuple-element.33.own_ref), channel_id=1, source_target_pairs={{0,1},{1,2},{2,3},{3,0},{4,5},{5,6},{6,7},{7,4},{8,9},{9,10},{10,1... | collective-permute-start | bytes 884744 | tf_op jit(solution)/shard_map/ppermute | solution.py:374
  35.5 21.5 %collective-permute-start.1 = (f32[192,384]{1,0:T(8,128)S(1)}, f32[192,384]{1,0:T(8,128)S(1)}, u32[]{:S(2)}, u32[]{:S(2)}) collective-permute-start(f32[192,384]{1,0:T(8,128)S(1)} %get-tuple-element.33.own_ref), channel_id=1, source_target_pairs={{0,2},{1,3},{2,0},{3,1},{4,6},{5,7},{6,4},{7,5},{8,10},{9,11},{10,... | collective-permute-start | bytes 884744 | tf_op jit(solution)/shard_map/ppermute | solution.py:374
  38.1 18.8 %collective-permute-start = (f32[192,384]{1,0:T(8,128)S(1)}, f32[192,384]{1,0:T(8,128)S(1)}, u32[]{:S(2)}, u32[]{:S(2)}) collective-permute-start(f32[192,384]{1,0:T(8,128)S(1)} %get-tuple-element.33.own_ref), channel_id=1, source_target_pairs={{0,3},{1,0},{2,1},{3,2},{4,7},{5,4},{6,5},{7,6},{8,11},{9,8},{10,9... | collective-permute-start | bytes 884744 | tf_op jit(solution)/shard_map/ppermute | solution.py:374
  45.5 20.0 %all-to-all-start.2 = ((f32[256,1,128]{2,1,0:T(1,128)}), f32[256,1,128]{2,1,0:T(1,128)S(1)}, u32[]{:S(2)}, u32[]{:S(2)}) async-start(f32[256,1,128]{2,1,0:T(1,128)} %get-tuple-element.29), calls=%async_computation.2 | async-start | bytes 262144 | tf_op jit(solution)/shard_map/all_to_all | solution.py:370
  82.7 14.7 %all-to-all-start.4 = ((f32[64,1,384]{2,1,0:T(1,128)}), f32[64,1,384]{2,1,0:T(1,128)S(1)}, u32[]{:S(2)}, u32[]{:S(2)}) async-start(f32[64,1,384]{2,1,0:T(1,128)} %get-tuple-element.38), calls=%async_computation.4 | async-start | bytes 196608 | tf_op jit(solution)/shard_map/all_to_all | solution.py:370
  87.2 4.3 %collective-permute-start.5 = (f32[1,128]{1,0:T(1,128)S(1)}, f32[1,128]{1,0:T(1,128)S(1)}, u32[]{:S(2)}, u32[]{:S(2)}) collective-permute-start(f32[1,128]{1,0:T(1,128)S(1)} %get-tuple-element.39.sum_ref), channel_id=1, source_target_pairs={{0,1},{1,2},{2,3},{3,0},{4,5},{5,6},{6,7},{7,4},{8,9},{9,10},{10,1... | collective-permute-start | bytes 1544 | tf_op jit(solution)/shard_map/ppermute | solution.py:374
  87.8 4.2 %collective-permute-start.4 = (f32[1,128]{1,0:T(1,128)S(1)}, f32[1,128]{1,0:T(1,128)S(1)}, u32[]{:S(2)}, u32[]{:S(2)}) collective-permute-start(f32[1,128]{1,0:T(1,128)S(1)} %get-tuple-element.39.sum_ref), channel_id=1, source_target_pairs={{0,2},{1,3},{2,0},{3,1},{4,6},{5,7},{6,4},{7,5},{8,10},{9,11},{10,... | collective-permute-start | bytes 1544 | tf_op jit(solution)/shard_map/ppermute | solution.py:374
  90.3 2.7 %collective-permute-start.3 = (f32[1,128]{1,0:T(1,128)S(1)}, f32[1,128]{1,0:T(1,128)S(1)}, u32[]{:S(2)}, u32[]{:S(2)}) collective-permute-start(f32[1,128]{1,0:T(1,128)S(1)} %get-tuple-element.39.sum_ref), channel_id=1, source_target_pairs={{0,3},{1,0},{2,1},{3,2},{4,7},{5,4},{6,5},{7,6},{8,11},{9,8},{10,9... | collective-permute-start | bytes 1544 | tf_op jit(solution)/shard_map/ppermute | solution.py:374

commit v6 on v5

--- a/solution.py
+++ b/solution.py
@@ -163,24 +163,18 @@
     solid_ref[...] = jnp.concatenate(pieces, axis=1)
 
 
-def weigh_kernel(in_ref, out_ref, weight_ref, place_ref, slot_ref, vertex_ref):
+def weigh_kernel(in_ref, place_ref, slot_ref, out_ref, weight_ref, vertex_ref):
     tiles = [in_ref[:, 0, at * 128 : at * 128 + 128] for at in range(6)]
     res = to_slots(tiles[:3])
     stiff = to_slots(tiles[3:])
-    lane = iota((256, 256), 1).astype(F32)
-    to_place = jnp.where(res[:, 7:8] == lane, 1.0, 0.0).astype(F32)
-    from_place = to_place.astype(BF16)
-    to_place = to_place.T.astype(BF16)
-    both = select_rows(to_place, jnp.concatenate([res, stiff], axis=1))
+    both = select_rows(place_ref[...], jnp.concatenate([res, stiff], axis=1))
     res = both[:, :128]
     stiff = both[:, 128:]
     weight = stiff / (stiff + partner(stiff))
-    back = select_rows(from_place, weight * (res + partner(res)))
+    back = select_rows(slot_ref[...], weight * (res + partner(res)))
     for k in range(3):
         out_ref[:, 0, k * 128 : k * 128 + 128] = from_slots(back, k)
     weight_ref[...] = weight
-    place_ref[...] = to_place
-    slot_ref[...] = from_place
     vertex_ref[...] = jnp.broadcast_to(res[:, 6:7], (256, 128)).T[0:1]
 
 
@@ -240,11 +234,22 @@
 
 
 def columns_kernel(
-    after_ref, inverse_hbm, corners_hbm, basis_hbm, out_ref, basis_ref, inverse, corners, sems
+    after_ref, inverse_hbm, corners_hbm, basis_hbm, assign_hbm, out_ref, basis_ref, place_ref,
+    slot_ref, inverse, corners, assign, sems,
 ):
     copies = fetch(
-        [inverse_hbm, corners_hbm, basis_hbm], [inverse, corners, basis_ref], sems
-    )
+        [inverse_hbm, corners_hbm, basis_hbm, assign_hbm],
+        [inverse, corners, basis_ref, assign],
+        sems,
+    )
+    copies[3].wait()
+    row = iota((256, 256), 0)
+    column = iota((256, 256), 1)
+    by_slot = jnp.where(row == assign[...], 1.0, 0.0).astype(BF16)
+    order = jnp.where(row == 4 * (column % 64) + column // 64, 1.0, 0.0).astype(BF16)
+    to_place = jnp.dot(by_slot, order, preferred_element_type=F32)
+    place_ref[...] = to_place.astype(BF16)
+    slot_ref[...] = to_place.T.astype(BF16)
     lane = iota((1, 128), 1)
     index = jnp.full((1, 128), -1, jnp.int32)
     copies[1].wait()
@@ -398,28 +403,27 @@
         residual.transpose(1, 0, 2),
         stiffness.transpose(1, 0, 2),
     )
-    own_columns, basis_here = call(
+    own_columns, basis_here, to_place, from_place = call(
         columns_kernel,
-        [VMEM, HBM, HBM, HBM],
-        [shaped(192, 384), VMEM((576, 768), BF16)],
+        [VMEM, HBM, HBM, HBM, HBM],
+        [
+            shaped(192, 384),
+            VMEM((576, 768), BF16),
+            VMEM((256, 256), BF16),
+            VMEM((256, 256), BF16),
+        ],
         "columns",
-        [VMEM((192, 768), F32), SMEM((4, 8), jnp.int32), dma((3,))],
-    )(solid_row, coarse_inverse, corners, basis_rows)
-    arrived, own_columns, basis_here = lax.optimization_barrier(
-        (exchange(packed, "sub"), own_columns, basis_here)
-    )
-    weighed, weight, to_place, from_place, vertex = call(
+        [VMEM((192, 768), F32), SMEM((4, 8), jnp.int32), VMEM((1, 256), jnp.int32), dma((4,))],
+    )(solid_row, coarse_inverse, corners, basis_rows, assign.reshape(1, 256))
+    arrived, own_columns, basis_here, to_place, from_place = lax.optimization_barrier(
+        (exchange(packed, "sub"), own_columns, basis_here, to_place, from_place)
+    )
+    weighed, weight, vertex = call(
         weigh_kernel,
-        [VMEM],
-        [
-            shaped(64, 1, 384),
-            shaped(256, 128),
-            shaped(256, 256, dtype=BF16),
-            shaped(256, 256, dtype=BF16),
-            shaped(1, 256),
-        ],
+        [VMEM] * 3,
+        [shaped(64, 1, 384), shaped(256, 128), shaped(1, 256)],
         "weigh",
-    )(arrived)
+    )(arrived, to_place, from_place)
     others = [from_ahead(own_columns, k) for k in (1, 2, 3)]
     received = exchange(weighed, "sub")
     message, rhs = call(

time: 98.6 us -> 98.6 us (level)
  transfers between devices with their start and end apart: 10 -> 10, of which waited for: 6 -> 6; matrix products, arithmetic and copies ran while one was open for 0% -> 0% of each run, Pallas kernels for 8% -> 9%
where the time goes in v6:
time: 98.6 us; the launch traced here: 98.2 us
  starting transfers between devices  39.6 us (40%)
  waiting for transfers between devices  27.3 us (28%)
  Pallas kernels  16.1 us (16%)
  blocking collectives  14.4 us (15%)
    all_to_all x4, starting transfers between devices, exchange(): return lax.all_to_all(values, axes, 0, 0)  30.2 us
    all_to_all x4, waiting for transfers between devices, exchange(): return lax.all_to_all(values, axes, 0, 0)  25.8 us
    all_to_all x1, blocking collectives, exchange(): return lax.all_to_all(values, axes, 0, 0)  14.4 us
    pallas_call x8, Pallas kernels, placed(): run(*(pltpu.with_memory_space_constraint(value, space) if space is HBM el...  11.8 us
    ppermute x6, starting transfers between devices, from_ahead(): return lax.ppermute(values, 'crs', [(y, (y - ahead) % 4) for y in range(4)])  9.33 us
    pallas_call x1, Pallas kernels, body(): pl.pallas_call(solve_kernel, grid=(STEPS,), in_specs=[whole, whole, whole...  4.34 us
  transfers between devices with their start and end apart: 10, of which 6 were waited for; matrix products, arithmetic and copies ran while one was open for 0% of the time, Pallas kernels for 9%

profile of v6, /device:TPU:1, one launch (start us, length us, event | category | flops | bytes accessed | tf_op | source)
XLA Modules:
  0.0 98.2 jit_solution(1982321118078642069)
XLA Ops:
  0.6 2.0 %pack.1 = (f32[64,1,768]{2,1,0:T(1,128)}, f32[1,128]{1,0:T(1,128)S(1)}) custom-call(s32[256]{0:T(256)} %assign_hbm.1, s32[4,8]{1,0:T(4,128)} %corners_hbm.3, s32[4,4,6]{2,1,0:T(4,128)} %bitcast.14, f32[6,4,768]{2,1,0:T(4,128)} %bitcast.12, f32[6,4,768]{2,1,0:T(4,128)} %bitcast.13), custom_call_target="tpu_custom_call" | custom-call | tf_op jit(solution)/shard_map/pack/pallas_call | solution.py:364
  2.6 13.0 %all-to-all-start = ((f32[64,1,768]{2,1,0:T(1,128)}), f32[64,1,768]{2,1,0:T(1,128)S(1)}, u32[]{:S(2)}, u32[]{:S(2)}) async-start(f32[64,1,768]{2,1,0:T(1,128)} %get-tuple-element.24), calls=%async_computation | async-start | bytes 393216 | tf_op jit(solution)/shard_map/all_to_all | solution.py:375
  15.6 2.0 %columns.1 = (f32[192,384]{1,0:T(8,128)S(1)}, bf16[576,768]{1,0:T(8,128)(2,1)S(1)}, bf16[256,256]{1,0:T(8,128)(2,1)S(1)}, bf16[256,256]{1,0:T(8,128)(2,1)S(1)}) custom-call(f32[1,128]{1,0:T(1,128)S(1)} %get-tuple-element.25.after_ref.solid_ref, f32[192,768]{1,0:T(8,128)} %inverse_hbm.1, s32[4,8]{1,0:T(4,128)} %corners_hbm.3, bf16[576,768]{1,0:T(8,128)(2,1)} %bitcast.11, ...), custom_call_target="tpu_custom_call" | custom-call | tf_op jit(solution)/shard_map/columns/pallas_call | solution.py:364
  17.7 8.9 %all-to-all-done.in_ref = f32[64,1,768]{2,1,0:T(1,128)S(1)} async-done(((f32[64,1,768]{2,1,0:T(1,128)}), f32[64,1,768]{2,1,0:T(1,128)S(1)}, u32[]{:S(2)}, u32[]{:S(2)}) %all-to-all-start) | async-done | bytes 196640 | tf_op jit(solution)/shard_map/all_to_all | solution.py:375
  26.6 1.8 %weigh.1 = (f32[64,1,384]{2,1,0:T(1,128)}, f32[256,128]{1,0:T(8,128)S(1)}, f32[1,256]{1,0:T(1,128)S(1)}) custom-call(f32[64,1,768]{2,1,0:T(1,128)S(1)} %all-to-all-done.in_ref, bf16[256,256]{1,0:T(8,128)(2,1)S(1)} %get-tuple-element.31.place_ref, bf16[256,256]{1,0:T(8,128)(2,1)S(1)} %get-tuple-element.32.slot_ref), custom_call_target="tpu_custom_call" | custom-call | tf_op jit(solution)/shard_map/weigh/pallas_call | solution.py:364
  28.3 5.7 %all-to-all-start.1 = ((f32[64,1,384]{2,1,0:T(1,128)}), f32[64,1,384]{2,1,0:T(1,128)S(1)}, u32[]{:S(2)}, u32[]{:S(2)}) async-start(f32[64,1,384]{2,1,0:T(1,128)} %get-tuple-element.33), calls=%async_computation.1 | async-start | bytes 196608 | tf_op jit(solution)/shard_map/all_to_all | solution.py:375
  34.0 1.4 %collective-permute-start.2 = (f32[192,384]{1,0:T(8,128)S(1)}, f32[192,384]{1,0:T(8,128)S(1)}, u32[]{:S(2)}, u32[]{:S(2)}) collective-permute-start(f32[192,384]{1,0:T(8,128)S(1)} %get-tuple-element.38.own_ref), channel_id=1, source_target_pairs={{0,1},{1,2},{2,3},{3,0},{4,5},{5,6},{6,7},{7,4},{8,9},{9,10},{10,1... | collective-permute-start | bytes 884744 | tf_op jit(solution)/shard_map/ppermute | solution.py:379
  35.4 2.6 %collective-permute-start.1 = (f32[192,384]{1,0:T(8,128)S(1)}, f32[192,384]{1,0:T(8,128)S(1)}, u32[]{:S(2)}, u32[]{:S(2)}) collective-permute-start(f32[192,384]{1,0:T(8,128)S(1)} %get-tuple-element.38.own_ref), channel_id=1, source_target_pairs={{0,2},{1,3},{2,0},{3,1},{4,6},{5,7},{6,4},{7,5},{8,10},{9,11},{10,... | collective-permute-start | bytes 884744 | tf_op jit(solution)/shard_map/ppermute | solution.py:379
  38.0 1.1 %collective-permute-start = (f32[192,384]{1,0:T(8,128)S(1)}, f32[192,384]{1,0:T(8,128)S(1)}, u32[]{:S(2)}, u32[]{:S(2)}) collective-permute-start(f32[192,384]{1,0:T(8,128)S(1)} %get-tuple-element.38.own_ref), channel_id=1, source_target_pairs={{0,3},{1,0},{2,1},{3,2},{4,7},{5,4},{6,5},{7,6},{8,11},{9,8},{10,9... | collective-permute-start | bytes 884744 | tf_op jit(solution)/shard_map/ppermute | solution.py:379
  39.1 5.1 %all-to-all-done.1.in_ref = f32[64,1,384]{2,1,0:T(1,128)S(1)} async-done(((f32[64,1,384]{2,1,0:T(1,128)}), f32[64,1,384]{2,1,0:T(1,128)S(1)}, u32[]{:S(2)}, u32[]{:S(2)}) %all-to-all-start.1) | async-done | bytes 98336 | tf_op jit(solution)/shard_map/all_to_all | solution.py:375
  44.2 1.3 %parts.1 = (f32[256,1,128]{2,1,0:T(1,128)}, bf16[768,128]{1,0:T(8,128)(2,1)S(1)}) custom-call(f32[64,1,384]{2,1,0:T(1,128)S(1)} %all-to-all-done.1.in_ref, f32[1,128]{1,0:T(1,128)S(1)} %get-tuple-element.25.after_ref.solid_ref, bf16[576,768]{1,0:T(8,128)(2,1)S(1)} %get-tuple-element.34.basis.basis_ref), custom_call_target="tpu_custom_call" | custom-call | tf_op jit(solution)/shard_map/parts/pallas_call | solution.py:364
  45.4 7.1 %all-to-all-start.2 = ((f32[256,1,128]{2,1,0:T(1,128)}), f32[256,1,128]{2,1,0:T(1,128)S(1)}, u32[]{:S(2)}, u32[]{:S(2)}) async-start(f32[256,1,128]{2,1,0:T(1,128)} %get-tuple-element.35), calls=%async_computation.2 | async-start | bytes 262144 | tf_op jit(solution)/shard_map/all_to_all | solution.py:375
  52.5 4.3 %solve.1 = (f32[192,128]{1,0:T(8,128)S(1)}, f32[1,128]{1,0:T(1,128)S(1)}) custom-call(f32[64,1,384]{2,1,0:T(1,128)S(1)} %all-to-all-done.1.in_ref, f32[1,128]{1,0:T(1,128)S(1)} %get-tuple-element.25.after_ref.solid_ref, bf16[768,128]{1,0:T(8,128)(2,1)S(1)} %get-tuple-element.36.after_ref.rhs, bf16[4608,768]{1,0:T(8,128)(2,1)} %bitcast.10), custom_call_target="tpu_custom_call" | custom-call | tf_op jit(solution)/shard_map/solve/pallas_call | solution.py:437
  56.9 0.0 collective-permute-done.2.three_ref
  56.9 0.0 collective-permute-done.1.two_ref
  56.9 0.0 collective-permute-done.one_ref
  56.9 1.1 %pick.1.picked_ref = f32[768,128]{1,0:T(8,128)S(1)} custom-call(bf16[768,128]{1,0:T(8,128)(2,1)S(1)} %get-tuple-element.36.after_ref.rhs, f32[1,256]{1,0:T(1,128)S(1)} %get-tuple-element.37.vertex_ref, f32[192,384]{1,0:T(8,128)S(1)} %get-tuple-element.38.own_ref, f32[192,384]{1,0:T(8,128)S(1)} %collective-permute-done.one_ref, ...), custom_call_target="tpu_custom_call" | custom-call | tf_op jit(solution)/shard_map/pick/pallas_call | solution.py:364
  58.0 7.4 %all-to-all-done.2.in_ref = f32[256,1,128]{2,1,0:T(1,128)S(1)} async-done(((f32[256,1,128]{2,1,0:T(1,128)}), f32[256,1,128]{2,1,0:T(1,128)S(1)}, u32[]{:S(2)}, u32[]{:S(2)}) %all-to-all-start.2) | async-done | bytes 131104 | tf_op jit(solution)/shard_map/all_to_all | solution.py:375
  65.4 1.4 %coarse.1 = f32[64,1,384]{2,1,0:T(1,128)S(1)} custom-call(f32[256,1,128]{2,1,0:T(1,128)S(1)} %all-to-all-done.2.in_ref, bf16[256,256]{1,0:T(8,128)(2,1)S(1)} %get-tuple-element.31.place_ref, f32[768,128]{1,0:T(8,128)S(1)} %pick.1.picked_ref, f32[192,128]{1,0:T(8,128)S(1)} %get-tuple-element.39.local_ref, f32[1,128]{1,0:T(1,128)S(1)} %get-tuple-element.40.inner_ref, ...), custom_call_target="tpu_custom_call" | custom-call | tf_op jit(solution)/shard_map/coarse/pallas_call | solution.py:364
  66.8 14.4 %all_to_all.25.in_ref = f32[64,1,384]{2,1,0:T(1,128)S(1)} all-to-all(f32[64,1,384]{2,1,0:T(1,128)S(1)} %coarse.1), channel_id=1, replica_groups=mesh['sub'=64,'crs'=4] {'sub'}, dimensions={0} | all-to-all | bytes 196608 | tf_op jit(solution)/shard_map/all_to_all | solution.py:375
  81.2 1.5 %average.1 = (f32[64,1,384]{2,1,0:T(1,128)}, f32[1,128]{1,0:T(1,128)S(1)}) custom-call(f32[64,1,384]{2,1,0:T(1,128)S(1)} %all_to_all.25.in_ref, bf16[256,256]{1,0:T(8,128)(2,1)S(1)} %get-tuple-element.31.place_ref, bf16[256,256]{1,0:T(8,128)(2,1)S(1)} %get-tuple-element.32.slot_ref, f32[256,128]{1,0:T(8,128)S(1)} %get-tuple-element.41.weight_ref), custom_call_target="tpu_custom_call" | custom-call | tf_op jit(solution)/shard_map/average/pallas_call | solution.py:364
  82.7 4.4 %all-to-all-start.4 = ((f32[64,1,384]{2,1,0:T(1,128)}), f32[64,1,384]{2,1,0:T(1,128)S(1)}, u32[]{:S(2)}, u32[]{:S(2)}) async-start(f32[64,1,384]{2,1,0:T(1,128)} %get-tuple-element.42), calls=%async_computation.4 | async-start | bytes 196608 | tf_op jit(solution)/shard_map/all_to_all | solution.py:375
  87.1 0.6 collective-permute-start.5
  87.8 2.5 %collective-permute-start.4 = (f32[1,128]{1,0:T(1,128)S(1)}, f32[1,128]{1,0:T(1,128)S(1)}, u32[]{:S(2)}, u32[]{:S(2)}) collective-permute-start(f32[1,128]{1,0:T(1,128)S(1)} %get-tuple-element.43.sum_ref), channel_id=1, source_target_pairs={{0,2},{1,3},{2,0},{3,1},{4,6},{5,7},{6,4},{7,5},{8,10},{9,11},{10,... | collective-permute-start | bytes 1544 | tf_op jit(solution)/shard_map/ppermute | solution.py:379
  90.3 1.1 %collective-permute-start.3 = (f32[1,128]{1,0:T(1,128)S(1)}, f32[1,128]{1,0:T(1,128)S(1)}, u32[]{:S(2)}, u32[]{:S(2)}) collective-permute-start(f32[1,128]{1,0:T(1,128)S(1)} %get-tuple-element.43.sum_ref), channel_id=1, source_target_pairs={{0,3},{1,0},{2,1},{3,2},{4,7},{5,4},{6,5},{7,6},{8,11},{9,8},{10,9... | collective-permute-start | bytes 1544 | tf_op jit(solution)/shard_map/ppermute | solution.py:379
  91.4 0.0 collective-permute-done.5.three_ref
  91.4 0.5 collective-permute-done.4.two_ref
  91.9 1.0 %collective-permute-done.3.one_ref = f32[1,128]{1,0:T(1,128)S(1)} collective-permute-done((f32[1,128]{1,0:T(1,128)S(1)}, f32[1,128]{1,0:T(1,128)S(1)}, u32[]{:S(2)}, u32[]{:S(2)}) %collective-permute-start.3) | collective-permute-done | bytes 544 | tf_op jit(solution)/shard_map/ppermute | solution.py:379
  93.0 4.4 %all-to-all-done.4.in_ref = f32[64,1,384]{2,1,0:T(1,128)S(1)} async-done(((f32[64,1,384]{2,1,0:T(1,128)}), f32[64,1,384]{2,1,0:T(1,128)S(1)}, u32[]{:S(2)}, u32[]{:S(2)}) %all-to-all-start.4) | async-done | bytes 98336 | tf_op jit(solution)/shard_map/all_to_all | solution.py:375
  97.4 0.8 unpack.1
Async XLA Ops:
  2.6 23.9 %all-to-all-start = ((f32[64,1,768]{2,1,0:T(1,128)}), f32[64,1,768]{2,1,0:T(1,128)S(1)}, u32[]{:S(2)}, u32[]{:S(2)}) async-start(f32[64,1,768]{2,1,0:T(1,128)} %get-tuple-element.24), calls=%async_computation | async-start | bytes 393216 | tf_op jit(solution)/shard_map/all_to_all | solution.py:375
  28.3 15.8 %all-to-all-start.1 = ((f32[64,1,384]{2,1,0:T(1,128)}), f32[64,1,384]{2,1,0:T(1,128)S(1)}, u32[]{:S(2)}, u32[]{:S(2)}) async-start(f32[64,1,384]{2,1,0:T(1,128)} %get-tuple-element.33), calls=%async_computation.1 | async-start | bytes 196608 | tf_op jit(solution)/shard_map/all_to_all | solution.py:375
  34.0 22.8 %collective-permute-start.2 = (f32[192,384]{1,0:T(8,128)S(1)}, f32[192,384]{1,0:T(8,128)S(1)}, u32[]{:S(2)}, u32[]{:S(2)}) collective-permute-start(f32[192,384]{1,0:T(8,128)S(1)} %get-tuple-element.38.own_ref), channel_id=1, source_target_pairs={{0,1},{1,2},{2,3},{3,0},{4,5},{5,6},{6,7},{7,4},{8,9},{9,10},{10,1... | collective-permute-start | bytes 884744 | tf_op jit(solution)/shard_map/ppermute | solution.py:379
  35.4 21.5 %collective-permute-start.1 = (f32[192,384]{1,0:T(8,128)S(1)}, f32[192,384]{1,0:T(8,128)S(1)}, u32[]{:S(2)}, u32[]{:S(2)}) collective-permute-start(f32[192,384]{1,0:T(8,128)S(1)} %get-tuple-element.38.own_ref), channel_id=1, source_target_pairs={{0,2},{1,3},{2,0},{3,1},{4,6},{5,7},{6,4},{7,5},{8,10},{9,11},{10,... | collective-permute-start | bytes 884744 | tf_op jit(solution)/shard_map/ppermute | solution.py:379
  38.0 18.8 %collective-permute-start = (f32[192,384]{1,0:T(8,128)S(1)}, f32[192,384]{1,0:T(8,128)S(1)}, u32[]{:S(2)}, u32[]{:S(2)}) collective-permute-start(f32[192,384]{1,0:T(8,128)S(1)} %get-tuple-element.38.own_ref), channel_id=1, source_target_pairs={{0,3},{1,0},{2,1},{3,2},{4,7},{5,4},{6,5},{7,6},{8,11},{9,8},{10,9... | collective-permute-start | bytes 884744 | tf_op jit(solution)/shard_map/ppermute | solution.py:379
  45.4 20.0 %all-to-all-start.2 = ((f32[256,1,128]{2,1,0:T(1,128)}), f32[256,1,128]{2,1,0:T(1,128)S(1)}, u32[]{:S(2)}, u32[]{:S(2)}) async-start(f32[256,1,128]{2,1,0:T(1,128)} %get-tuple-element.35), calls=%async_computation.2 | async-start | bytes 262144 | tf_op jit(solution)/shard_map/all_to_all | solution.py:375
  82.7 14.7 %all-to-all-start.4 = ((f32[64,1,384]{2,1,0:T(1,128)}), f32[64,1,384]{2,1,0:T(1,128)S(1)}, u32[]{:S(2)}, u32[]{:S(2)}) async-start(f32[64,1,384]{2,1,0:T(1,128)} %get-tuple-element.42), calls=%async_computation.4 | async-start | bytes 196608 | tf_op jit(solution)/shard_map/all_to_all | solution.py:375
  87.1 4.3 %collective-permute-start.5 = (f32[1,128]{1,0:T(1,128)S(1)}, f32[1,128]{1,0:T(1,128)S(1)}, u32[]{:S(2)}, u32[]{:S(2)}) collective-permute-start(f32[1,128]{1,0:T(1,128)S(1)} %get-tuple-element.43.sum_ref), channel_id=1, source_target_pairs={{0,1},{1,2},{2,3},{3,0},{4,5},{5,6},{6,7},{7,4},{8,9},{9,10},{10,1... | collective-permute-start | bytes 1544 | tf_op jit(solution)/shard_map/ppermute | solution.py:379
  87.8 4.2 %collective-permute-start.4 = (f32[1,128]{1,0:T(1,128)S(1)}, f32[1,128]{1,0:T(1,128)S(1)}, u32[]{:S(2)}, u32[]{:S(2)}) collective-permute-start(f32[1,128]{1,0:T(1,128)S(1)} %get-tuple-element.43.sum_ref), channel_id=1, source_target_pairs={{0,2},{1,3},{2,0},{3,1},{4,6},{5,7},{6,4},{7,5},{8,10},{9,11},{10,... | collective-permute-start | bytes 1544 | tf_op jit(solution)/shard_map/ppermute | solution.py:379
  90.3 2.7 %collective-permute-start.3 = (f32[1,128]{1,0:T(1,128)S(1)}, f32[1,128]{1,0:T(1,128)S(1)}, u32[]{:S(2)}, u32[]{:S(2)}) collective-permute-start(f32[1,128]{1,0:T(1,128)S(1)} %get-tuple-element.43.sum_ref), channel_id=1, source_target_pairs={{0,3},{1,0},{2,1},{3,2},{4,7},{5,4},{6,5},{7,6},{8,11},{9,8},{10,9... | collective-permute-start | bytes 1544 | tf_op jit(solution)/shard_map/ppermute | solution.py:379
